TPU v7x, 32 devices: a whole 2x2x4 slice. The times are simulated.
32 devices in a mesh: ctx: 4 (over x, core), dp: 2 (over y), tp: 4 (over z).
Axes of the slice: x: 2, y: 2, z: 4, core: 2. Of those that a mesh axis runs over, the one named last changes fastest.
Arguments:
- token_ids: int32 [4, 4], replicated, may hold values from 0 to 50279
- decode_prompt: int32 [4], replicated, may hold values from 0 to 3, as said below
- embedding: bfloat16 [50280, 4096], P('dp', ('ctx', 'tp')), may hold values from -6 to 6
- norm_gain: float32 [4096], replicated, may hold values from 0.1 to 1.9
- w_zx: bfloat16 [2, 128, 64, 4096], P(None, ('tp', 'ctx')), may hold values from -0.09375 to 0.09375
- w_bcdt: bfloat16 [4096, 384], P(None, ('ctx', 'tp')), may hold values from -0.09375 to 0.09375
- conv_x_weight: float32 [4, 128, 64], P(None, ('tp', 'ctx')), may hold values from -3 to 3
- conv_x_bias: float32 [128, 64], P(('tp', 'ctx')), may hold values from -3 to 3
- conv_bc_weight: float32 [4, 256], replicated, may hold values from -3 to 3
- conv_bc_bias: float32 [256], replicated, may hold values from -3 to 3
- dt_bias: float32 [128], P(('tp', 'ctx')), may hold values from -4 to -1
- a_log: float32 [128], P(('tp', 'ctx')), may hold values from 0 to 2.7
- d_skip: float32 [128], P(('tp', 'ctx')), may hold values from 0.5 to 1.5
- gate_norm_gain: float32 [128, 64], P(('tp', 'ctx')), may hold values from 0.1 to 1.9
- w_out: bfloat16 [128, 64, 4096], P(('tp', 'ctx')), may hold values from -0.0625 to 0.0625
- state_parts: bfloat16 [4, 4, 128, 64, 128], P('ctx', 'dp', 'tp'), may hold values from -6 to 6
- seg_rate: float32 [4, 4, 128], P('ctx', 'dp', 'tp'), may hold values from 0 to 4
- x_tail: bfloat16 [4, 3, 128, 64], P('dp', None, ('tp', 'ctx')), may hold values from -6 to 6
- bc_tail: bfloat16 [4, 3, 256], P('dp'), may hold values from -6 to 6
Outputs:
- mixer_out: bfloat16 [4, 4, 4096], P(None, 'dp', ('ctx', 'tp'))
- final_state: float32 [4, 128, 64, 128], P('dp', ('tp', 'ctx'))
Inputs may be any that keep to these rules, and one draw needn't show every extreme that they name: decode_prompt is a permutation of the prompts; slot s is decoded by dp group s // 2, and prompt q is held by dp group q // 2; the 2 prompts held by one dp group are decoded by 2 different dp groups.
All inputs are finite; a program needn't handle non-finite values.
Results may differ from a plain program's by a relative error of at most 0.02.
Values may be sent and summed in bfloat16 or wider, within the bound.
A program may use at most 64 MiB of HBM per device.

v0:
```python
import functools

import jax
import jax.numpy as jnp
from jax import lax
from jax.experimental import pallas as pl
from jax.experimental.pallas import tpu as pltpu
from jax.sharding import PartitionSpec as P

HEADS = 128
HEAD_DIM = 64


epsilon = 1e-05


def entering(shard, axis, combine, identity):
    count, here = (lax.axis_size(axis), lax.axis_index(axis))
    everything = lax.all_gather(shard, axis)
    start = jnp.broadcast_to(jnp.asarray(identity, shard.dtype), shard.shape)

    def step(k, before):
        at = count - 1 - k
        reached = at > here
        new = combine(before, everything[at])
        return jnp.where(reached, new, before)

    return lax.fori_loop(0, count, step, start)


def rms_scale(values, gain):
    return values * lax.rsqrt(jnp.mean(values * values, axis=-1, keepdims=True) + epsilon) * gain


def select_rows(picker, values):
    return jnp.tensordot(picker, values, axes=1, precision=lax.Precision.HIGHEST)


def add_rates(earlier, later_one):
    return earlier + later_one


def per_device(
    token_ids,
    decode_prompt,
    embedding,
    norm_gain,
    w_zx,
    w_bcdt,
    conv_x_weight,
    conv_x_bias,
    conv_bc_weight,
    conv_bc_bias,
    dt_bias,
    a_log,
    d_skip,
    gate_norm_gain,
    w_out,
    state_parts,
    seg_rate,
    x_tail,
    bc_tail,
):
    group = lax.axis_index("dp")
    local_count = state_parts.shape[1]
    slot_count = decode_prompt.shape[0]
    head_count = w_zx.shape[1]
    state_width = conv_bc_bias.shape[0] // 2
    after_rates = entering(seg_rate, "ctx", add_rates, jnp.zeros_like(seg_rate))
    seg_weight = jnp.exp(-after_rates[0])
    scaled = seg_weight[:, :, None, None] * state_parts[0].astype(jnp.float32)
    channel_sums = lax.psum_scatter(
        scaled.astype(jnp.bfloat16), "ctx", scatter_dimension=2, tiled=True
    ).astype(jnp.float32)
    combined = lax.all_to_all(
        channel_sums.astype(jnp.bfloat16), "ctx", split_axis=1, concat_axis=2, tiled=True
    ).astype(channel_sums.dtype)
    tails_x = x_tail.astype(jnp.float32)
    tails_bc = bc_tail.astype(jnp.float32)
    own_slots = lax.dynamic_slice_in_dim(decode_prompt, group * local_count, local_count)
    prompt_ids = jnp.arange(slot_count, dtype=jnp.int32)
    every_state, every_x, every_bc = (
        lax.all_gather(combined.astype(jnp.bfloat16), "dp", axis=0, tiled=True).astype(
            combined.dtype
        ),
        lax.all_gather(tails_x.astype(jnp.bfloat16), "dp", axis=0, tiled=True).astype(
            tails_x.dtype
        ),
        lax.all_gather(tails_bc.astype(jnp.bfloat16), "dp", axis=0, tiled=True).astype(
            tails_bc.dtype
        ),
    )
    picker = (own_slots[:, None] == prompt_ids[None, :]).astype(jnp.float32)
    ssm_state = select_rows(picker, every_state)
    x_window = select_rows(picker, every_x)
    bc_window = select_rows(picker, every_bc)
    vocab_rows = embedding.shape[0]
    holder = (decode_prompt[:, None] == prompt_ids[None, :]).astype(jnp.int32)
    slot_tokens = jnp.sum(token_ids[:, None, :] * holder[None], axis=2)
    offset_tokens = slot_tokens - group * vocab_rows
    inside = (offset_tokens >= 0) & (offset_tokens < vocab_rows)
    looked = jnp.take(embedding, jnp.clip(offset_tokens, 0, vocab_rows - 1), axis=0)
    partial_rows = jnp.where(inside[..., None], looked.astype(jnp.float32), 0.0)
    own_rows = lax.psum_scatter(
        partial_rows.astype(jnp.bfloat16), "dp", scatter_dimension=1, tiled=True
    )
    embedded = lax.all_gather(own_rows, ("ctx", "tp"), axis=2, tiled=True)
    steps_count = embedded.shape[0]
    flat_rows = embedded.reshape(-1, embedded.shape[2]).astype(jnp.float32)
    normed = rms_scale(flat_rows, norm_gain).astype(jnp.bfloat16)
    projected = jnp.einsum("rd,khed->krhe", normed, w_zx, preferred_element_type=jnp.float32)
    projected = projected.reshape(
        2, steps_count, local_count, projected.shape[2], projected.shape[3]
    )
    columns = lax.all_gather(
        jnp.dot(normed, w_bcdt, preferred_element_type=jnp.float32),
        ("ctx", "tp"),
        axis=1,
        tiled=True,
    )
    columns = columns.reshape(steps_count, local_count, -1)
    head_block = lax.axis_index("tp") * lax.axis_size("ctx") + lax.axis_index("ctx")
    head_start = 2 * state_width + head_block * head_count
    dt_raw = lax.dynamic_slice_in_dim(columns, head_start, head_count, 2)
    decay_rate = -jnp.exp(a_log)
    gated_steps = []
    for moment in range(steps_count):
        x_window = jnp.concatenate([x_window, projected[1, moment][:, None]], axis=1)
        bc_window = jnp.concatenate(
            [bc_window, columns[moment, :, None, : 2 * state_width]], axis=1
        )
        x_conv = jax.nn.silu(jnp.einsum("pkhe,khe->phe", x_window, conv_x_weight) + conv_x_bias)
        bc_conv = jax.nn.silu(jnp.einsum("pkn,kn->pn", bc_window, conv_bc_weight) + conv_bc_bias)
        step_size = jax.nn.softplus(dt_raw[moment] + dt_bias)
        retain = jnp.exp(step_size * decay_rate)
        ssm_state = (
            retain[:, :, None, None] * ssm_state
            + (step_size[:, :, None] * x_conv)[:, :, :, None] * bc_conv[:, None, None, :state_width]
        )
        output = (
            jnp.einsum("phen,pn->phe", ssm_state, bc_conv[:, state_width:])
            + d_skip[None, :, None] * x_conv
        )
        gated_steps.append(output * jax.nn.silu(projected[0, moment]))
        x_window = x_window[:, 1:]
        bc_window = bc_window[:, 1:]
    gated_all = jnp.stack(gated_steps)
    local_squares = jnp.sum(gated_all * gated_all, axis=(2, 3))
    total_squares = lax.psum(local_squares, ("ctx", "tp"))
    inverse = lax.rsqrt(total_squares / (HEADS * HEAD_DIM) + epsilon)
    normed_out = (gated_all * inverse[:, :, None, None] * gate_norm_gain).astype(jnp.bfloat16)
    partial_out = jnp.einsum("tphe,hed->tpd", normed_out, w_out, preferred_element_type=jnp.float32)
    outer_sum = lax.psum_scatter(
        partial_out.astype(jnp.bfloat16), "ctx", scatter_dimension=2, tiled=True
    ).astype(jnp.float32)
    mixed = lax.psum_scatter(outer_sum, "tp", scatter_dimension=2, tiled=True)
    return (mixed.astype(jnp.bfloat16), ssm_state)


HI = lax.Precision.HIGHEST
F32 = jnp.float32
BF16 = jnp.bfloat16


def f32_dot(a, b):
    return jnp.dot(a, b, precision=HI, preferred_element_type=F32)


def nt_dot(a, b):
    return lax.dot_general(a, b, (((1,), (1,)), ((), ())), preferred_element_type=F32)


def silu(v):
    return v / (1.0 + jnp.exp(-v))


def softplus(v):
    return jnp.maximum(v, 0.0) + jnp.log1p(jnp.exp(-jnp.abs(v)))


ROW_TILE = 16


def gather_kernel(steps, slots, groups, tok_ref, dec_ref, emb_ref, out_ref, buf, tail, sems, tail_sem):
    vocab = emb_ref.shape[0]
    whole = vocab // ROW_TILE * ROW_TILE
    base = lax.axis_index("dp") * vocab
    per_group = slots // groups
    tail_copy = None
    if whole < vocab:
        tail_copy = pltpu.make_async_copy(emb_ref.at[pl.ds(whole, vocab - whole)], tail, tail_sem)
        tail_copy.start()
    copies = []
    where = []
    for s in range(slots):
        q = dec_ref[s]
        for t in range(steps):
            row = tok_ref[t, q] - base
            clipped = jnp.clip(row, 0, vocab - 1)
            start = jnp.minimum(clipped // ROW_TILE * ROW_TILE, whole - ROW_TILE)
            start = pl.multiple_of(start, ROW_TILE)
            i = s * steps + t
            copy = pltpu.make_async_copy(emb_ref.at[pl.ds(start, ROW_TILE)], buf.at[i], sems.at[i])
            copy.start()
            copies.append(copy)
            where.append((row, start))
    if tail_copy is not None:
        tail_copy.wait()
    for copy in copies:
        copy.wait()
    rows = lax.broadcasted_iota(jnp.int32, (ROW_TILE, 1), 0)
    for g in range(groups):
        picked = []
        for t in range(steps):
            for j in range(per_group):
                i = (g * per_group + j) * steps + t
                row, start = where[i]
                value = jnp.sum(
                    jnp.where(rows == row - start, buf[i].astype(F32), 0.0), axis=0, keepdims=True
                )
                if tail_copy is not None:
                    trows = lax.broadcasted_iota(jnp.int32, (vocab - whole, 1), 0)
                    value += jnp.sum(
                        jnp.where(trows == row - whole, tail[...].astype(F32), 0.0),
                        axis=0,
                        keepdims=True,
                    )
                picked.append(value)
        out_ref[g] = jnp.concatenate(picked, axis=0).astype(BF16)


def mixer_kernel(
    sizes,
    dec_ref,
    part_ref,
    seg_ref,
    xt_ref,
    bt_ref,
    gain_hbm,
    cxw_hbm,
    cxb_hbm,
    cbw_hbm,
    cbb_hbm,
    dtb_hbm,
    alog_hbm,
    skip_hbm,
    gg_hbm,
    wzx_hbm,
    wbc_hbm,
    wout_hbm,
    state_hbm,
    mixed_ref,
    final_hbm,
    gain_ref,
    cxw_ref,
    cxb_ref,
    cbw_ref,
    cbb_ref,
    dtb_ref,
    alog_ref,
    skip_ref,
    gg_ref,
    final_ref,
    pair_recv,
    pair_send,
    wzx,
    wbc,
    wout,
    state_in,
    state_send,
    state_recv,
    emb_recv,
    seg_recv,
    xt_recv,
    bt_recv,
    col_send,
    col_recv,
    sq_send,
    sq_recv,
    out_send,
    out_recv,
    start_state,
    xfull,
    bcfull,
    gated_ref,
    load_sems,
    small_sems,
    own_sems,
    final_sem,
    pair_sems,
    seg_mate,
    seg_own,
    emb_sems,
    state_sems,
    seg_sems,
    xt_sems,
    bt_sems,
    col_sems,
    sq_sems,
    out_sems,
):
    n_ctx, n_dp, n_tp, total_heads = sizes
    c, d, p = lax.axis_index("ctx"), lax.axis_index("dp"), lax.axis_index("tp")
    mine = c * n_tp + p
    steps, per, feats = mixed_ref.shape
    rows = steps * per
    heads, dim = cxb_ref.shape
    chans = heads * dim
    width = cbb_ref.shape[1]
    state_n = width // 2
    taps = cxw_ref.shape[0]
    model = gain_ref.shape[1]
    tp_heads = seg_ref.shape[-1]
    n_cols = wbc_hbm.shape[0]
    all_cols = n_cols * n_ctx * n_tp

    def peer(offset):
        dc, dd, dt = offset
        return lax.rem(c + dc, n_ctx), lax.rem(d + dd, n_dp), lax.rem(p + dt, n_tp)

    def device(offset):
        a, b, e = peer(offset)
        return {"ctx": a, "dp": b, "tp": e}

    everyone = [
        (a, b, e) for a in range(n_ctx) for b in range(n_dp) for e in range(n_tp) if a + b + e
    ]
    everyone.sort(key=lambda o: -(min(o[2], n_tp - o[2]) * 4 + o[1] * 2 + o[0]))
    group = [o for o in everyone if o[1] == 0]
    routed = [o for o in everyone if o[2] == 0]
    across = [o for o in everyone if o[0] == 0 and o[2] == 0]

    barrier = pltpu.get_barrier_semaphore()
    for o in everyone:
        pl.semaphore_signal(
            barrier, inc=1, device_id=device(o), device_id_type=pl.DeviceIdType.MESH
        )

    loads = []
    half = wzx_hbm.shape[0] // 2
    pairs = (
        (state_hbm, state_in),
        (wbc_hbm, wbc),
        (wzx_hbm.at[pl.ds(half, half)], wzx.at[pl.ds(half, half)]),
        (wzx_hbm.at[pl.ds(0, half)], wzx.at[pl.ds(0, half)]),
        (wout_hbm, wout),
    )
    for i, (source, target) in enumerate(pairs):
        load = pltpu.make_async_copy(source, target, load_sems.at[i])
        load.start()
        loads.append(load)

    small_pairs = (
        (gain_hbm, gain_ref),
        (cxw_hbm, cxw_ref),
        (cxb_hbm, cxb_ref),
        (cbw_hbm, cbw_ref),
        (cbb_hbm, cbb_ref),
        (dtb_hbm, dtb_ref),
        (alog_hbm, alog_ref),
        (skip_hbm, skip_ref),
        (gg_hbm, gg_ref),
    )
    smalls = []
    for i, (source, target) in enumerate(small_pairs):
        load = pltpu.make_async_copy(source, target, small_sems.at[i])
        load.start()
        smalls.append(load)
    owns = []
    for source, target in (
        (part_ref.at[d], emb_recv.at[d, mine]),
        (seg_ref.at[0], seg_recv.at[d, c]),
        (xt_ref, xt_recv.at[d]),
        (bt_ref, bt_recv.at[d]),
        (seg_ref.at[0], seg_own),
    ):
        load = pltpu.make_async_copy(source, target, own_sems.at[len(owns)])
        load.start()
        owns.append(load)

    def send(source, target, sems, slot, offset):
        copy = pltpu.make_async_remote_copy(
            src_ref=source,
            dst_ref=target,
            send_sem=sems.at[0, slot],
            recv_sem=sems.at[1, slot],
            device_id=device(offset),
            device_id_type=pl.DeviceIdType.MESH,
        )
        copy.start()
        return copy

    loads[0].wait()
    picks = []
    for b in range(n_dp):
        target_group = lax.rem(d + b, n_dp)
        pick = jnp.int32(0)
        for j in range(per):
            local = dec_ref[target_group * per + j] - d * per
            pick += jnp.where((local >= 0) & (local < per), local, 0)
        state_send[b] = state_in[pick]
        picks.append(pick)

    col_send[...] = jnp.zeros_like(col_send)

    pl.semaphore_wait(barrier, len(everyone))

    emb_copies = [
        send(part_ref.at[peer(o)[1]], emb_recv.at[d, mine], emb_sems, i, o)
        for i, o in enumerate(everyone)
    ]
    parity = lax.rem(c, 2)
    mate = c + 1 - 2 * parity
    blocks = [(a, b) for a in reversed(range(n_ctx // 2)) for b in reversed(range(n_dp))]

    def to_mate(source, target, slot):
        copy = pltpu.make_async_remote_copy(
            src_ref=source,
            dst_ref=target,
            send_sem=pair_sems.at[0, slot],
            recv_sem=pair_sems.at[1, slot],
            device_id={"ctx": mate, "dp": d, "tp": p},
            device_id_type=pl.DeviceIdType.MESH,
        )
        copy.start()
        return copy

    mate_copy = to_mate(seg_ref.at[0], seg_mate, len(blocks))
    pair_copies = []
    for slot, (a, b) in enumerate(blocks):
        first = pl.multiple_of(lax.rem(mate + 2 * a, n_ctx) * chans, chans)
        source = state_send.at[b, pl.ds(first, chans)]
        pair_copies.append(to_mate(source, pair_recv.at[b, a], slot))
    pair_copies.append(mate_copy)
    seg_copies = [send(seg_ref.at[0], seg_recv.at[d, c], seg_sems, i, o) for i, o in enumerate(routed)]
    xt_copies = [send(xt_ref, xt_recv.at[d], xt_sems, i, o) for i, o in enumerate(across)]
    bt_copies = [send(bt_ref, bt_recv.at[d], bt_sems, i, o) for i, o in enumerate(across)]

    fold = (
        lax.broadcasted_iota(jnp.int32, (dim, chans), 0)
        == lax.rem(lax.broadcasted_iota(jnp.int32, (dim, chans), 1), dim)
    ).astype(F32)
    head_rows = lax.broadcasted_iota(jnp.int32, (heads, chans), 0) == lax.div(
        lax.broadcasted_iota(jnp.int32, (heads, chans), 1), dim
    )

    def flat(value):
        return jnp.sum(jnp.where(head_rows, f32_dot(value, fold), 0.0), axis=0, keepdims=True)

    def spread(value, first):
        count = value.shape[1]
        chosen = (
            lax.broadcasted_iota(jnp.int32, (count, chans), 0)
            == first + lax.div(lax.broadcasted_iota(jnp.int32, (count, chans), 1), dim)
        ).astype(F32)
        return f32_dot(value, chosen)

    owns[4].wait()
    mate_copy.wait_recv()
    shrink = []
    for b in range(n_dp):
        row = pl.ds(picks[b], 1)
        shrink.append(jnp.exp(-jnp.where(parity == 0, seg_mate[row, :], seg_own[row, :])))
    ones = [jnp.ones((1, tp_heads), F32)] * n_dp
    shrink = jnp.concatenate(shrink + ones, axis=0)
    shrink_cols = [
        jnp.transpose(spread(shrink, lax.rem(c + 2 * a, n_ctx) * heads)) for a in range(n_ctx // 2)
    ]
    state_copies = []
    for slot, (a, b) in enumerate(blocks):
        pair_copies[slot].wait_recv()
        first = pl.multiple_of(lax.rem(c + 2 * a, n_ctx) * chans, chans)
        here = state_send[b, pl.ds(first, chans), :].astype(F32)
        there = pair_recv[b, a].astype(F32)
        factor = shrink_cols[a][:, b : b + 1]
        even = jnp.where(parity == 0, here, there)
        odd = jnp.where(parity == 0, there, here)
        added = (factor * even + odd).astype(BF16)
        target = state_recv.at[d, lax.div(c, 2)]
        if a + b:
            pair_send[b, a] = added
            state_copies.append(send(pair_send.at[b, a], target, state_sems, slot, (2 * a, b, 0)))
        else:
            state_recv[d, lax.div(c, 2)] = added

    for load in smalls:
        load.wait()
    tap_rows = [flat(cxw_ref[k]) for k in range(taps)]
    bias_row = flat(cxb_ref[...])
    gate_row = flat(gg_ref[...])
    dtb_row = spread(dtb_ref[...], 0)
    rate_row = -jnp.exp(spread(alog_ref[...], 0))
    skip_row = spread(skip_ref[...], 0)

    owns[0].wait()
    for copy in emb_copies:
        copy.wait_recv()
    pieces = []
    for i in range(n_ctx * n_tp):
        piece = emb_recv[0, i].astype(F32)
        for g in range(1, n_dp):
            piece += emb_recv[g, i].astype(F32)
        pieces.append(piece)
    embedded = jnp.concatenate(pieces, axis=1)
    scale = lax.rsqrt(jnp.sum(embedded * embedded, axis=1, keepdims=True) / model + epsilon)
    normed = (embedded * scale * gain_ref[...]).astype(BF16)
    loads[1].wait()
    col_send[:, 0:n_cols] = nt_dot(normed, wbc[...])
    col_copies = [send(col_send, col_recv.at[mine], col_sems, i, o) for i, o in enumerate(group)]
    col_recv[mine] = col_send[...]
    loads[2].wait()
    x_rows = nt_dot(normed, wzx[half : 2 * half, :])
    loads[3].wait()
    z_gate = silu(nt_dot(normed, wzx[0:half, :]))

    owns[2].wait()
    owns[3].wait()
    for copy in xt_copies + bt_copies:
        copy.wait_recv()
    holders = [lax.div(dec_ref[d * per + j], per) for j in range(per)]
    places = [lax.rem(dec_ref[d * per + j], per) for j in range(per)]
    plane_rows = lax.broadcasted_iota(jnp.int32, (per, 1), 0)
    for k in range(taps - 1):
        for j in range(per):
            r = k * per + j
            xfull[r : r + 1, :] = flat(xt_recv[holders[j], places[j], k].astype(F32))
            plane = bt_recv[holders[j], k].astype(F32)
            bcfull[r : r + 1, :] = jnp.sum(
                jnp.where(plane_rows == places[j], plane, 0.0), axis=0, keepdims=True
            )
    lead = (taps - 1) * per
    xfull[lead : lead + rows, :] = x_rows
    conv = bias_row
    for k in range(taps):
        conv = conv + tap_rows[k] * xfull[k * per : k * per + rows, :]
    xc = silu(conv)

    owns[1].wait()
    for copy in seg_copies:
        copy.wait_recv()
    weights = []
    for j in range(per):
        after = jnp.zeros((1, tp_heads), F32)
        ordered = []
        row = pl.ds(places[j], 1)
        for m in reversed(range(n_ctx // 2)):
            ordered.append(jnp.exp(-after))
            for k in (2 * m + 1, 2 * m):
                after = after + seg_recv[holders[j], k, row, :]
        weights.extend(reversed(ordered))
    weight_cols = jnp.transpose(spread(jnp.concatenate(weights, axis=0), c * heads))
    for copy in state_copies:
        copy.wait_recv()
    for j in range(per):
        begin = None
        for m in range(n_ctx // 2):
            r = j * (n_ctx // 2) + m
            term = weight_cols[:, r : r + 1] * state_recv[holders[j], m].astype(F32)
            begin = term if begin is None else begin + term
        start_state[j] = begin

    for copy in col_copies:
        copy.wait_recv()
    wide_pad = jnp.zeros((rows, all_cols - col_send.shape[1]), F32)
    columns = jnp.zeros((rows, all_cols), F32)
    for i in range(n_ctx * n_tp):
        wide = jnp.concatenate([col_recv[i], wide_pad], axis=1)
        columns = columns + (pltpu.roll(wide, n_cols * i, 1) if i else wide)
    bcfull[lead : lead + rows, :] = columns[:, :width]
    conv = cbb_ref[...]
    for k in range(taps):
        conv = conv + cbw_ref[k : k + 1, :] * bcfull[k * per : k * per + rows, :]
    bcc = silu(conv)
    b_all, c_all = bcc[:, :state_n], bcc[:, state_n:]
    head_first = (p * n_ctx + c) * heads
    step_size = softplus(spread(columns[:, width:], head_first) + dtb_row)
    log_keep = step_size * rate_row
    driven = step_size * xc

    row_slot = lax.rem(lax.broadcasted_iota(jnp.int32, (rows, 1), 0), per)
    from_start = jnp.zeros((rows, chans), F32)
    c_low = c_all.astype(BF16)
    for j in range(per):
        from_start += jnp.where(row_slot == j, nt_dot(c_low, start_state[j].astype(BF16)), 0.0)

    def at(value, t):
        return value[t * per : (t + 1) * per]

    total = jnp.zeros((per, chans), F32)
    sums = []
    for t in range(steps):
        total = total + at(log_keep, t)
        sums.append(total)
    for t in range(steps):
        y = jnp.exp(sums[t]) * at(from_start, t) + skip_row * at(xc, t)
        for s in range(t + 1):
            overlap = jnp.sum(at(b_all, s) * at(c_all, t), axis=1, keepdims=True)
            term = at(driven, s) * overlap
            y = y + (term if s == t else jnp.exp(sums[t] - sums[s]) * term)
        gated_ref[t * per : (t + 1) * per, :] = y
    gated = gated_ref[...] * z_gate
    squares = jnp.sum(gated * gated, axis=1, keepdims=True)
    sq_send[...] = jnp.broadcast_to(squares, sq_send.shape)
    sq_copies = [send(sq_send, sq_recv.at[mine], sq_sems, i, o) for i, o in enumerate(group)]
    sq_recv[mine] = sq_send[...]

    loads[4].wait()
    partial = jnp.dot((gated * gate_row).astype(BF16), wout[...], preferred_element_type=F32)
    for i in range(n_ctx * n_tp):
        out_send[i] = partial[:, i * feats : (i + 1) * feats].astype(BF16)
    out_copies = []
    for i, o in enumerate(group):
        pc, _, pp = peer(o)
        out_copies.append(send(out_send.at[pc * n_tp + pp], out_recv.at[mine], out_sems, i, o))
    out_recv[mine] = out_send[mine]

    late = [jnp.exp(sums[-1] - sums[t]) * at(driven, t) for t in range(steps)]
    flat_rows = jnp.concatenate(late + [jnp.exp(sums[-1])] * (rows // per), axis=0)
    tall = jnp.transpose(flat_rows)
    for j in range(per):
        b_own = jnp.where(row_slot == j, b_all, 0.0)
        final_ref[j] = (
            tall[:, rows + j : rows + j + 1] * start_state[j] + f32_dot(tall[:, :rows], b_own)
        )

    final_copy = pltpu.make_async_copy(final_ref, final_hbm, final_sem)
    final_copy.start()

    for copy in sq_copies + out_copies:
        copy.wait_recv()
    total_squares = sq_recv[0]
    mixed = out_recv[0].astype(F32)
    for i in range(1, n_ctx * n_tp):
        total_squares = total_squares + sq_recv[i]
        mixed = mixed + out_recv[i].astype(F32)
    inverse = lax.rsqrt(total_squares[:, 0:1] / (total_heads * dim) + epsilon)
    mixed = mixed * inverse
    for t in range(steps):
        mixed_ref[t] = at(mixed, t).astype(BF16)
    for copy in (
        emb_copies + seg_copies + pair_copies + xt_copies + bt_copies + state_copies + col_copies + sq_copies
        + out_copies
    ):
        copy.wait_send()
    final_copy.wait()


def tail_kernel(mixed_in, final_in, mixed_out, final_out, mixed_buf, final_buf, in_sems, out_sems):
    moves = [(mixed_in, mixed_buf, mixed_out)]
    cuts = 4 if final_in.shape[1] % 32 == 0 else 1
    size = final_in.shape[1] // cuts
    for j in range(final_in.shape[0]):
        for k in range(cuts):
            piece = (j, pl.ds(k * size, size))
            moves.append((final_in.at[piece], final_buf.at[piece], final_out.at[piece]))
    moves = moves[1:] + moves[:1]
    inward = [pltpu.make_async_copy(a, b, in_sems.at[i]) for i, (a, b, _) in enumerate(moves)]
    outward = [pltpu.make_async_copy(b, e, out_sems.at[i]) for i, (_, b, e) in enumerate(moves)]
    for copy in inward:
        copy.start()
    for first, second in zip(inward, outward):
        first.wait()
        second.start()
    for copy in outward:
        copy.wait()


def kernel_device(
    sizes,
    token_ids,
    decode_prompt,
    embedding,
    norm_gain,
    w_zx,
    w_bcdt,
    conv_x_weight,
    conv_x_bias,
    conv_bc_weight,
    conv_bc_bias,
    dt_bias,
    a_log,
    d_skip,
    gate_norm_gain,
    w_out,
    state_parts,
    seg_rate,
    x_tail,
    bc_tail,
):
    n_ctx, n_dp, n_tp, _ = sizes
    steps = token_ids.shape[0]
    slots = decode_prompt.shape[0]
    per = state_parts.shape[1]
    rows = steps * per
    vocab, feats = embedding.shape
    heads, dim, model = w_zx.shape[1:]
    chans = heads * dim
    tp_heads, state_n = state_parts.shape[2], state_parts.shape[4]
    world, ring = n_ctx * n_dp * n_tp, n_ctx * n_tp
    smem = pl.BlockSpec(memory_space=pltpu.SMEM)
    vmem = pl.BlockSpec(memory_space=pltpu.VMEM)
    anywhere = pl.BlockSpec(memory_space=pl.ANY)
    rest = max(1, vocab % ROW_TILE)
    part = pl.pallas_call(
        functools.partial(gather_kernel, steps, slots, n_dp),
        out_shape=jax.ShapeDtypeStruct((n_dp, rows, feats), BF16),
        in_specs=[smem, smem, anywhere],
        out_specs=vmem,
        scratch_shapes=[
            pltpu.VMEM((steps * slots, ROW_TILE, feats), BF16),
            pltpu.VMEM((rest, feats), BF16),
            pltpu.SemaphoreType.DMA((steps * slots,)),
            pltpu.SemaphoreType.DMA,
        ],
        name="gather_rows",
    )(token_ids, decode_prompt, embedding)
    sem = pltpu.SemaphoreType.DMA
    wide = 2 * state_n
    full_rows = -(-(conv_x_weight.shape[0] - 1 + steps) * per // 8) * 8
    smalls = (
        norm_gain[None],
        conv_x_weight,
        conv_x_bias,
        conv_bc_weight,
        conv_bc_bias[None],
        dt_bias[None],
        a_log[None],
        d_skip[None],
        gate_norm_gain,
    )
    bc_planes = jnp.swapaxes(bc_tail, 0, 1)
    outs = (
        jax.ShapeDtypeStruct((steps, per, feats), BF16),
        jax.ShapeDtypeStruct((per, chans, state_n), F32),
    )
    pairs = n_ctx // 2
    mixed, final = pl.pallas_call(
        functools.partial(mixer_kernel, sizes),
        out_shape=outs,
        in_specs=[smem] + [anywhere] * 17,
        out_specs=(vmem, anywhere),
        scratch_shapes=[
            *[pltpu.VMEM(small.shape, small.dtype) for small in smalls],
            pltpu.VMEM((per, chans, state_n), F32),
            pltpu.VMEM((n_dp, pairs, chans, state_n), BF16),
            pltpu.VMEM((n_dp, pairs, chans, state_n), BF16),
            pltpu.VMEM((2 * chans, model), BF16),
            pltpu.VMEM(w_bcdt.shape[::-1], BF16),
            pltpu.VMEM((chans, model), BF16),
            pltpu.VMEM((per, tp_heads * dim, state_n), BF16),
            pltpu.VMEM((n_dp, tp_heads * dim, state_n), BF16),
            pltpu.VMEM((n_dp, pairs, chans, state_n), BF16),
            pltpu.VMEM((n_dp, ring, rows, feats), BF16),
            pltpu.VMEM((n_dp, n_ctx, per, tp_heads), F32),
            pltpu.VMEM((n_dp,) + x_tail.shape, BF16),
            pltpu.VMEM((n_dp,) + bc_planes.shape, BF16),
            pltpu.VMEM((rows, 128), F32),
            pltpu.VMEM((ring, rows, 128), F32),
            pltpu.VMEM((rows, 128), F32),
            pltpu.VMEM((ring, rows, 128), F32),
            pltpu.VMEM((ring, rows, feats), BF16),
            pltpu.VMEM((ring, rows, feats), BF16),
            pltpu.VMEM((per, chans, state_n), F32),
            pltpu.VMEM((full_rows, chans), F32),
            pltpu.VMEM((full_rows, wide), F32),
            pltpu.VMEM((rows, chans), F32),
            sem((5,)),
            sem((len(smalls),)),
            sem((5,)),
            sem,
            sem((2, n_dp * pairs + 1)),
            pltpu.VMEM((per, tp_heads), F32),
            pltpu.VMEM((per, tp_heads), F32),
            sem((2, world)),
            sem((2, n_dp * pairs)),
            sem((2, n_ctx * n_dp)),
            sem((2, n_dp)),
            sem((2, n_dp)),
            sem((2, ring)),
            sem((2, ring)),
            sem((2, ring)),
        ],
        compiler_params=pltpu.CompilerParams(
            collective_id=0, has_side_effects=True, vmem_limit_bytes=56 * 1024 * 1024
        ),
        name="mixer",
    )(
        decode_prompt,
        part,
        seg_rate,
        x_tail,
        bc_planes,
        *smalls,
        w_zx.reshape(2 * chans, model),
        w_bcdt.T,
        w_out.reshape(chans, model),
        state_parts.reshape(per, tp_heads * dim, state_n),
    )
    mixed, final = pl.pallas_call(
        tail_kernel,
        out_shape=outs,
        in_specs=[anywhere] * 2,
        out_specs=(anywhere, anywhere),
        scratch_shapes=[
            pltpu.VMEM(outs[0].shape, BF16),
            pltpu.VMEM(outs[1].shape, F32),
            sem((4 * per + 1,)),
            sem((4 * per + 1,)),
        ],
        name="tail",
    )(mixed, final)
    return mixed, final.reshape(per, heads, dim, state_n)


def choose_device(sizes, *args):
    embedding, w_zx, w_bcdt = args[2], args[4], args[5]
    heads, dim = w_zx.shape[1:3]
    fits = (
        embedding.shape[1] % 128 == 0
        and sizes[0] % 2 == 0
        and (heads * dim) % 128 == 0
        and w_bcdt.shape[1] <= 128
        and embedding.shape[0] >= ROW_TILE
    )
    if fits:
        return kernel_device(sizes, *args)
    return per_device(*args)


def solution(mesh):
    sizes = (mesh.shape["ctx"], mesh.shape["dp"], mesh.shape["tp"], HEADS)
    return jax.shard_map(
        functools.partial(choose_device, sizes),
        mesh=mesh,
        in_specs=(
            P(),
            P(),
            P("dp", ("ctx", "tp")),
            P(),
            P(None, ("tp", "ctx"), None, None),
            P(None, ("ctx", "tp")),
            P(None, ("tp", "ctx"), None),
            P(("tp", "ctx"), None),
            P(),
            P(),
            P(("tp", "ctx")),
            P(("tp", "ctx")),
            P(("tp", "ctx")),
            P(("tp", "ctx"), None),
            P(("tp", "ctx"), None, None),
            P("ctx", "dp", "tp", None, None),
            P("ctx", "dp", "tp"),
            P("dp", None, ("tp", "ctx"), None),
            P("dp", None, None),
        ),
        out_specs=(P(None, "dp", ("ctx", "tp")), P("dp", ("tp", "ctx"), None, None)),
        check_vma=False,
    )
```

profile of v0, /device:TPU:0, one launch (start us, length us, event | category | flops | bytes accessed | tf_op | source)
XLA Modules:
  0.0 32.0 jit_solution(1662370961259430982)
XLA Ops:
  0.6 2.6 %gather_rows.1.part_ref = bf16[2,8,256]{2,1,0:T(8,128)(2,1)} custom-call(s32[4,4]{1,0:T(4,128)} %tok_ref.1, s32[4]{0:T(128)} %dec_ref.3, bf16[25140,256]{1,0:T(8,128)(2,1)} %emb_ref.1), custom_call_target="tpu_custom_call" | custom-call | tf_op jit(solution)/shard_map/gather_rows/pallas_call | solution.py:704
  3.3 26.9 %mixer.1 = (bf16[4,2,256]{2,1,0:T(2,128)(2,1)}, f32[2,512,128]{2,1,0:T(8,128)}) custom-call(s32[4]{0:T(128)} %dec_ref.3, bf16[2,8,256]{2,1,0:T(8,128)(2,1)} %gather_rows.1.part_ref, f32[1,2,32]{2,1,0:T(2,128)} %seg_ref.1, bf16[2,3,8,64]{3,2,1,0:T(8,128)(2,1)} %xt_ref.1, bf16[3,2,256]{2,1,0:T(2,128)(2,1)} %bitcast.16, f32[1,4096]{1,0:T(1,128)} %bitcast.15, ...), custom_call_target="tpu_custom_call" | custom-call | tf_op jit(solution)/shard_map/mixer/pallas_call | solution.py:737
  30.2 1.9 %tail.1 = (bf16[4,2,256]{2,1,0:T(2,128)(2,1)}, f32[2,512,128]{2,1,0:T(8,128)}) custom-call(bf16[4,2,256]{2,1,0:T(2,128)(2,1)} %get-tuple-element.6.mixed_in, f32[2,512,128]{2,1,0:T(8,128)} %get-tuple-element.7.final_in), custom_call_target="tpu_custom_call" | custom-call | tf_op jit(solution)/shard_map/tail/pallas_call | solution.py:799
where the time goes:
time: 32.3 us; the launch traced here: 32 us
  Pallas kernels  31.4 us (97%)
  between operations  0.65 us (2%)
    pallas_call x1, Pallas kernels, kernel_device(): pl.pallas_call(functools.partial(mixer_kernel, sizes), out_shape=outs, in...  26.9 us
    pallas_call x1, Pallas kernels, kernel_device(): pl.pallas_call(functools.partial(gather_kernel, steps, slots, n_dp), out_...  2.64 us
    pallas_call x1, Pallas kernels, kernel_device(): pl.pallas_call(tail_kernel, out_shape=outs, in_specs=[anywhere] * 2, out_...  1.85 us

commit v1 on v0

--- a/solution.py
+++ b/solution.py
@@ -181,7 +181,11 @@
 ROW_TILE = 16
 
 
-def gather_kernel(steps, slots, groups, tok_ref, dec_ref, emb_ref, out_ref, buf, tail, sems, tail_sem):
+def drain(ref, sem):
+    pltpu.make_async_copy(ref, ref, sem).wait()
+
+
+def gather_kernel(steps, slots, groups, tok_ref, dec_ref, emb_ref, out_ref, buf, tail, sem, tail_sem):
     vocab = emb_ref.shape[0]
     whole = vocab // ROW_TILE * ROW_TILE
     base = lax.axis_index("dp") * vocab
@@ -190,7 +194,6 @@
     if whole < vocab:
         tail_copy = pltpu.make_async_copy(emb_ref.at[pl.ds(whole, vocab - whole)], tail, tail_sem)
         tail_copy.start()
-    copies = []
     where = []
     for s in range(slots):
         q = dec_ref[s]
@@ -200,14 +203,11 @@
             start = jnp.minimum(clipped // ROW_TILE * ROW_TILE, whole - ROW_TILE)
             start = pl.multiple_of(start, ROW_TILE)
             i = s * steps + t
-            copy = pltpu.make_async_copy(emb_ref.at[pl.ds(start, ROW_TILE)], buf.at[i], sems.at[i])
-            copy.start()
-            copies.append(copy)
+            pltpu.make_async_copy(emb_ref.at[pl.ds(start, ROW_TILE)], buf.at[i], sem).start()
             where.append((row, start))
     if tail_copy is not None:
         tail_copy.wait()
-    for copy in copies:
-        copy.wait()
+    drain(buf, sem)
     rows = lax.broadcasted_iota(jnp.int32, (ROW_TILE, 1), 0)
     for g in range(groups):
         picked = []
@@ -231,11 +231,11 @@
 
 def mixer_kernel(
     sizes,
-    dec_ref,
+    dec_hbm,
     part_ref,
-    seg_ref,
-    xt_ref,
-    bt_ref,
+    seg_hbm,
+    xt_hbm,
+    bt_hbm,
     gain_hbm,
     cxw_hbm,
     cxb_hbm,
@@ -250,7 +250,8 @@
     wout_hbm,
     state_hbm,
     mixed_ref,
-    final_hbm,
+    final_ref,
+    dec_ref,
     gain_ref,
     cxw_ref,
     cxb_ref,
@@ -260,7 +261,6 @@
     alog_ref,
     skip_ref,
     gg_ref,
-    final_ref,
     pair_recv,
     pair_send,
     wzx,
@@ -269,8 +269,12 @@
     state_in,
     state_send,
     state_recv,
-    emb_recv,
+    plane_recv,
+    line_send,
+    line_recv,
     seg_recv,
+    seg_mate,
+    seg_own,
     xt_recv,
     bt_recv,
     col_send,
@@ -286,12 +290,11 @@
     load_sems,
     small_sems,
     own_sems,
-    final_sem,
     pair_sems,
-    seg_mate,
-    seg_own,
-    emb_sems,
+    mate_sems,
     state_sems,
+    plane_sems,
+    line_sems,
     seg_sems,
     xt_sems,
     bt_sems,
@@ -302,6 +305,8 @@
     n_ctx, n_dp, n_tp, total_heads = sizes
     c, d, p = lax.axis_index("ctx"), lax.axis_index("dp"), lax.axis_index("tp")
     mine = c * n_tp + p
+    here_plane = d * n_ctx + c
+    ring, plane = n_ctx * n_tp, n_dp * n_ctx
     steps, per, feats = mixed_ref.shape
     rows = steps * per
     heads, dim = cxb_ref.shape
@@ -310,34 +315,47 @@
     state_n = width // 2
     taps = cxw_ref.shape[0]
     model = gain_ref.shape[1]
-    tp_heads = seg_ref.shape[-1]
+    tp_heads = seg_recv.shape[-1]
     n_cols = wbc_hbm.shape[0]
     all_cols = n_cols * n_ctx * n_tp
+    half = wzx_hbm.shape[0] // 2
+    mirror = n_tp == 4
 
     def peer(offset):
         dc, dd, dt = offset
-        return lax.rem(c + dc, n_ctx), lax.rem(d + dd, n_dp), lax.rem(p + dt, n_tp)
+        away = lax.rem(p + dt, n_tp)
+        if mirror and dt != n_tp // 2:
+            away = n_tp - 1 - (p if dt == 1 else lax.rem(p + n_tp // 2, n_tp))
+        return lax.rem(c + dc, n_ctx), lax.rem(d + dd, n_dp), away if dt else p
 
     def device(offset):
         a, b, e = peer(offset)
         return {"ctx": a, "dp": b, "tp": e}
 
-    everyone = [
-        (a, b, e) for a in range(n_ctx) for b in range(n_dp) for e in range(n_tp) if a + b + e
-    ]
-    everyone.sort(key=lambda o: -(min(o[2], n_tp - o[2]) * 4 + o[1] * 2 + o[0]))
-    group = [o for o in everyone if o[1] == 0]
-    routed = [o for o in everyone if o[2] == 0]
-    across = [o for o in everyone if o[0] == 0 and o[2] == 0]
+    far = [1, 2, 3] if mirror else list(range(n_tp - 1, 0, -1))
+    routed = [(a, b, 0) for a in reversed(range(n_ctx)) for b in reversed(range(n_dp)) if a + b]
+    line = [(0, 0, e) for e in far]
+    group = [(a, 0, e) for e in far + [0] for a in reversed(range(n_ctx)) if a + e]
+    across = [(0, b, 0) for b in range(1, n_dp)]
 
     barrier = pltpu.get_barrier_semaphore()
-    for o in everyone:
+    for o in line + routed:
         pl.semaphore_signal(
             barrier, inc=1, device_id=device(o), device_id_type=pl.DeviceIdType.MESH
         )
 
+    owns = []
+    for source, target in (
+        (dec_hbm, dec_ref),
+        (seg_hbm.at[0], seg_own),
+        (xt_hbm, xt_recv.at[d]),
+        (bt_hbm, bt_recv.at[d]),
+    ):
+        load = pltpu.make_async_copy(source, target, own_sems.at[len(owns)])
+        load.start()
+        owns.append(load)
     loads = []
-    half = wzx_hbm.shape[0] // 2
+    smalls = []
     pairs = (
         (state_hbm, state_in),
         (wbc_hbm, wbc),
@@ -345,11 +363,6 @@
         (wzx_hbm.at[pl.ds(0, half)], wzx.at[pl.ds(0, half)]),
         (wout_hbm, wout),
     )
-    for i, (source, target) in enumerate(pairs):
-        load = pltpu.make_async_copy(source, target, load_sems.at[i])
-        load.start()
-        loads.append(load)
-
     small_pairs = (
         (gain_hbm, gain_ref),
         (cxw_hbm, cxw_ref),
@@ -361,36 +374,46 @@
         (skip_hbm, skip_ref),
         (gg_hbm, gg_ref),
     )
-    smalls = []
-    for i, (source, target) in enumerate(small_pairs):
-        load = pltpu.make_async_copy(source, target, small_sems.at[i])
+
+    def fetch(source, target, sem, into):
+        load = pltpu.make_async_copy(source, target, sem)
         load.start()
-        smalls.append(load)
-    owns = []
-    for source, target in (
-        (part_ref.at[d], emb_recv.at[d, mine]),
-        (seg_ref.at[0], seg_recv.at[d, c]),
-        (xt_ref, xt_recv.at[d]),
-        (bt_ref, bt_recv.at[d]),
-        (seg_ref.at[0], seg_own),
-    ):
-        load = pltpu.make_async_copy(source, target, own_sems.at[len(owns)])
-        load.start()
-        owns.append(load)
-
-    def send(source, target, sems, slot, offset):
-        copy = pltpu.make_async_remote_copy(
+        into.append(load)
+
+    fetch(*pairs[0], load_sems.at[0], loads)
+    for i, pair in enumerate(small_pairs):
+        fetch(*pair, small_sems.at[i], smalls)
+    for i, pair in enumerate(pairs[1:]):
+        fetch(*pair, load_sems.at[i + 1], loads)
+
+    def send(source, target, send_sem, recv_sem, place):
+        pltpu.make_async_remote_copy(
             src_ref=source,
             dst_ref=target,
-            send_sem=sems.at[0, slot],
-            recv_sem=sems.at[1, slot],
-            device_id=device(offset),
+            send_sem=send_sem,
+            recv_sem=recv_sem,
+            device_id=place,
             device_id_type=pl.DeviceIdType.MESH,
-        )
-        copy.start()
-        return copy
-
-    loads[0].wait()
+        ).start()
+
+    col_send[...] = jnp.zeros_like(col_send)
+
+    pl.semaphore_wait(barrier, len(line) + len(routed))
+
+    for o in routed:
+        send(part_ref.at[peer(o)[1]], plane_recv.at[here_plane], plane_sems.at[0], plane_sems.at[1], device(o))
+    plane_recv[here_plane] = part_ref[d]
+
+    owns[0].wait()
+    owns[1].wait()
+    parity = lax.rem(c, 2)
+    mate = {"ctx": c + 1 - 2 * parity, "dp": d, "tp": p}
+    half_ctx = n_ctx // 2
+    blocks = [(a, b) for a in reversed(range(half_ctx)) for b in reversed(range(n_dp))]
+    seg_recv[here_plane] = seg_own[...]
+    send(seg_own, seg_mate, mate_sems.at[0], mate_sems.at[1], mate)
+    for o in routed:
+        send(seg_own, seg_recv.at[here_plane], seg_sems.at[0], seg_sems.at[1], device(o))
     picks = []
     for b in range(n_dp):
         target_group = lax.rem(d + b, n_dp)
@@ -398,43 +421,17 @@
         for j in range(per):
             local = dec_ref[target_group * per + j] - d * per
             pick += jnp.where((local >= 0) & (local < per), local, 0)
-        state_send[b] = state_in[pick]
         picks.append(pick)
-
-    col_send[...] = jnp.zeros_like(col_send)
-
-    pl.semaphore_wait(barrier, len(everyone))
-
-    emb_copies = [
-        send(part_ref.at[peer(o)[1]], emb_recv.at[d, mine], emb_sems, i, o)
-        for i, o in enumerate(everyone)
-    ]
-    parity = lax.rem(c, 2)
-    mate = c + 1 - 2 * parity
-    blocks = [(a, b) for a in reversed(range(n_ctx // 2)) for b in reversed(range(n_dp))]
-
-    def to_mate(source, target, slot):
-        copy = pltpu.make_async_remote_copy(
-            src_ref=source,
-            dst_ref=target,
-            send_sem=pair_sems.at[0, slot],
-            recv_sem=pair_sems.at[1, slot],
-            device_id={"ctx": mate, "dp": d, "tp": p},
-            device_id_type=pl.DeviceIdType.MESH,
-        )
-        copy.start()
-        return copy
-
-    mate_copy = to_mate(seg_ref.at[0], seg_mate, len(blocks))
-    pair_copies = []
+    loads[0].wait()
     for slot, (a, b) in enumerate(blocks):
-        first = pl.multiple_of(lax.rem(mate + 2 * a, n_ctx) * chans, chans)
-        source = state_send.at[b, pl.ds(first, chans)]
-        pair_copies.append(to_mate(source, pair_recv.at[b, a], slot))
-    pair_copies.append(mate_copy)
-    seg_copies = [send(seg_ref.at[0], seg_recv.at[d, c], seg_sems, i, o) for i, o in enumerate(routed)]
-    xt_copies = [send(xt_ref, xt_recv.at[d], xt_sems, i, o) for i, o in enumerate(across)]
-    bt_copies = [send(bt_ref, bt_recv.at[d], bt_sems, i, o) for i, o in enumerate(across)]
+        first = pl.multiple_of(lax.rem(mate["ctx"] + 2 * a, n_ctx) * chans, chans)
+        state_send[slot] = state_in[picks[b], pl.ds(first, chans), :]
+        send(state_send.at[slot], pair_recv.at[slot], pair_sems.at[len(blocks)], pair_sems.at[slot], mate)
+    owns[2].wait()
+    owns[3].wait()
+    for o in across:
+        send(xt_recv.at[d], xt_recv.at[d], xt_sems.at[0], xt_sems.at[1], device(o))
+        send(bt_recv.at[d], bt_recv.at[d], bt_sems.at[0], bt_sems.at[1], device(o))
 
     fold = (
         lax.broadcasted_iota(jnp.int32, (dim, chans), 0)
@@ -455,8 +452,17 @@
         ).astype(F32)
         return f32_dot(value, chosen)
 
-    owns[4].wait()
-    mate_copy.wait_recv()
+    drain(plane_recv.at[pl.ds(0, plane - 1)], plane_sems.at[1])
+    for i in range(n_ctx):
+        piece = plane_recv[i].astype(F32)
+        for g in range(1, n_dp):
+            piece += plane_recv[g * n_ctx + i].astype(F32)
+        line_send[i] = piece.astype(BF16)
+    for o in line:
+        send(line_send, line_recv.at[p], line_sems.at[0], line_sems.at[1], device(o))
+    line_recv[p] = line_send[...]
+
+    drain(seg_mate, mate_sems.at[1])
     shrink = []
     for b in range(n_dp):
         row = pl.ds(picks[b], 1)
@@ -464,24 +470,23 @@
     ones = [jnp.ones((1, tp_heads), F32)] * n_dp
     shrink = jnp.concatenate(shrink + ones, axis=0)
     shrink_cols = [
-        jnp.transpose(spread(shrink, lax.rem(c + 2 * a, n_ctx) * heads)) for a in range(n_ctx // 2)
+        jnp.transpose(spread(shrink, lax.rem(c + 2 * a, n_ctx) * heads)) for a in range(half_ctx)
     ]
-    state_copies = []
     for slot, (a, b) in enumerate(blocks):
-        pair_copies[slot].wait_recv()
+        drain(pair_recv.at[slot], pair_sems.at[slot])
         first = pl.multiple_of(lax.rem(c + 2 * a, n_ctx) * chans, chans)
-        here = state_send[b, pl.ds(first, chans), :].astype(F32)
-        there = pair_recv[b, a].astype(F32)
+        here = state_in[picks[b], pl.ds(first, chans), :].astype(F32)
+        there = pair_recv[slot].astype(F32)
         factor = shrink_cols[a][:, b : b + 1]
         even = jnp.where(parity == 0, here, there)
         odd = jnp.where(parity == 0, there, here)
         added = (factor * even + odd).astype(BF16)
-        target = state_recv.at[d, lax.div(c, 2)]
+        target = state_recv.at[d * half_ctx + lax.div(c, 2)]
         if a + b:
-            pair_send[b, a] = added
-            state_copies.append(send(pair_send.at[b, a], target, state_sems, slot, (2 * a, b, 0)))
+            pair_send[slot] = added
+            send(pair_send.at[slot], target, state_sems.at[0], state_sems.at[1], device((2 * a, b, 0)))
         else:
-            state_recv[d, lax.div(c, 2)] = added
+            state_recv[d * half_ctx + lax.div(c, 2)] = added
 
     for load in smalls:
         load.wait()
@@ -492,42 +497,49 @@
     rate_row = -jnp.exp(spread(alog_ref[...], 0))
     skip_row = spread(skip_ref[...], 0)
 
-    owns[0].wait()
-    for copy in emb_copies:
-        copy.wait_recv()
-    pieces = []
-    for i in range(n_ctx * n_tp):
-        piece = emb_recv[0, i].astype(F32)
-        for g in range(1, n_dp):
-            piece += emb_recv[g, i].astype(F32)
-        pieces.append(piece)
+    holders = [lax.div(dec_ref[d * per + j], per) for j in range(per)]
+    places = [lax.rem(dec_ref[d * per + j], per) for j in range(per)]
+    for sems, ref in ((xt_sems, xt_recv), (bt_sems, bt_recv)):
+        if across:
+            drain(ref.at[pl.ds(0, n_dp - 1)], sems.at[1])
+    plane_rows = lax.broadcasted_iota(jnp.int32, (per, 1), 0)
+    for k in range(taps - 1):
+        for j in range(per):
+            r = k * per + j
+            xfull[r : r + 1, :] = flat(xt_recv[holders[j], places[j], k].astype(F32))
+            tail = bt_recv[holders[j], k].astype(F32)
+            bcfull[r : r + 1, :] = jnp.sum(
+                jnp.where(plane_rows == places[j], tail, 0.0), axis=0, keepdims=True
+            )
+
+    drain(seg_recv.at[pl.ds(0, plane - 1)], seg_sems.at[1])
+    weights = []
+    for j in range(per):
+        after = jnp.zeros((1, tp_heads), F32)
+        ordered = []
+        row = pl.ds(places[j], 1)
+        for m in reversed(range(half_ctx)):
+            ordered.append(jnp.exp(-after))
+            for k in (2 * m + 1, 2 * m):
+                after = after + seg_recv[holders[j] * n_ctx + k, row, :]
+        weights.extend(reversed(ordered))
+    weight_cols = jnp.transpose(spread(jnp.concatenate(weights, axis=0), c * heads))
+
+    drain(line_recv.at[pl.ds(0, n_tp - 1)], line_sems.at[1])
+    pieces = [line_recv[e, i].astype(F32) for i in range(n_ctx) for e in range(n_tp)]
     embedded = jnp.concatenate(pieces, axis=1)
     scale = lax.rsqrt(jnp.sum(embedded * embedded, axis=1, keepdims=True) / model + epsilon)
     normed = (embedded * scale * gain_ref[...]).astype(BF16)
     loads[1].wait()
     col_send[:, 0:n_cols] = nt_dot(normed, wbc[...])
-    col_copies = [send(col_send, col_recv.at[mine], col_sems, i, o) for i, o in enumerate(group)]
+    for o in group:
+        send(col_send, col_recv.at[mine], col_sems.at[0], col_sems.at[1], device(o))
     col_recv[mine] = col_send[...]
     loads[2].wait()
     x_rows = nt_dot(normed, wzx[half : 2 * half, :])
     loads[3].wait()
     z_gate = silu(nt_dot(normed, wzx[0:half, :]))
 
-    owns[2].wait()
-    owns[3].wait()
-    for copy in xt_copies + bt_copies:
-        copy.wait_recv()
-    holders = [lax.div(dec_ref[d * per + j], per) for j in range(per)]
-    places = [lax.rem(dec_ref[d * per + j], per) for j in range(per)]
-    plane_rows = lax.broadcasted_iota(jnp.int32, (per, 1), 0)
-    for k in range(taps - 1):
-        for j in range(per):
-            r = k * per + j
-            xfull[r : r + 1, :] = flat(xt_recv[holders[j], places[j], k].astype(F32))
-            plane = bt_recv[holders[j], k].astype(F32)
-            bcfull[r : r + 1, :] = jnp.sum(
-                jnp.where(plane_rows == places[j], plane, 0.0), axis=0, keepdims=True
-            )
     lead = (taps - 1) * per
     xfull[lead : lead + rows, :] = x_rows
     conv = bias_row
@@ -535,35 +547,19 @@
         conv = conv + tap_rows[k] * xfull[k * per : k * per + rows, :]
     xc = silu(conv)
 
-    owns[1].wait()
-    for copy in seg_copies:
-        copy.wait_recv()
-    weights = []
-    for j in range(per):
-        after = jnp.zeros((1, tp_heads), F32)
-        ordered = []
-        row = pl.ds(places[j], 1)
-        for m in reversed(range(n_ctx // 2)):
-            ordered.append(jnp.exp(-after))
-            for k in (2 * m + 1, 2 * m):
-                after = after + seg_recv[holders[j], k, row, :]
-        weights.extend(reversed(ordered))
-    weight_cols = jnp.transpose(spread(jnp.concatenate(weights, axis=0), c * heads))
-    for copy in state_copies:
-        copy.wait_recv()
+    drain(state_recv.at[pl.ds(0, n_dp * half_ctx - 1)], state_sems.at[1])
     for j in range(per):
         begin = None
-        for m in range(n_ctx // 2):
-            r = j * (n_ctx // 2) + m
-            term = weight_cols[:, r : r + 1] * state_recv[holders[j], m].astype(F32)
+        for m in range(half_ctx):
+            r = j * half_ctx + m
+            term = weight_cols[:, r : r + 1] * state_recv[holders[j] * half_ctx + m].astype(F32)
             begin = term if begin is None else begin + term
         start_state[j] = begin
 
-    for copy in col_copies:
-        copy.wait_recv()
+    drain(col_recv.at[pl.ds(0, ring - 1)], col_sems.at[1])
     wide_pad = jnp.zeros((rows, all_cols - col_send.shape[1]), F32)
     columns = jnp.zeros((rows, all_cols), F32)
-    for i in range(n_ctx * n_tp):
+    for i in range(ring):
         wide = jnp.concatenate([col_recv[i], wide_pad], axis=1)
         columns = columns + (pltpu.roll(wide, n_cols * i, 1) if i else wide)
     bcfull[lead : lead + rows, :] = columns[:, :width]
@@ -600,18 +596,21 @@
         gated_ref[t * per : (t + 1) * per, :] = y
     gated = gated_ref[...] * z_gate
     squares = jnp.sum(gated * gated, axis=1, keepdims=True)
-    sq_send[...] = jnp.broadcast_to(squares, sq_send.shape)
-    sq_copies = [send(sq_send, sq_recv.at[mine], sq_sems, i, o) for i, o in enumerate(group)]
+    diagonal = lax.broadcasted_iota(jnp.int32, (rows, 128), 0) == lax.broadcasted_iota(
+        jnp.int32, (rows, 128), 1
+    )
+    sq_send[...] = jnp.sum(jnp.where(diagonal, squares, 0.0), axis=0, keepdims=True)
+    for o in group:
+        send(sq_send, sq_recv.at[mine], sq_sems.at[0], sq_sems.at[1], device(o))
     sq_recv[mine] = sq_send[...]
 
     loads[4].wait()
     partial = jnp.dot((gated * gate_row).astype(BF16), wout[...], preferred_element_type=F32)
-    for i in range(n_ctx * n_tp):
+    for i in range(ring):
         out_send[i] = partial[:, i * feats : (i + 1) * feats].astype(BF16)
-    out_copies = []
-    for i, o in enumerate(group):
+    for o in group:
         pc, _, pp = peer(o)
-        out_copies.append(send(out_send.at[pc * n_tp + pp], out_recv.at[mine], out_sems, i, o))
+        send(out_send.at[pc * n_tp + pp], out_recv.at[mine], out_sems.at[0], out_sems.at[1], device(o))
     out_recv[mine] = out_send[mine]
 
     late = [jnp.exp(sums[-1] - sums[t]) * at(driven, t) for t in range(steps)]
@@ -623,46 +622,32 @@
             tall[:, rows + j : rows + j + 1] * start_state[j] + f32_dot(tall[:, :rows], b_own)
         )
 
-    final_copy = pltpu.make_async_copy(final_ref, final_hbm, final_sem)
-    final_copy.start()
-
-    for copy in sq_copies + out_copies:
-        copy.wait_recv()
+    drain(plane_recv.at[pl.ds(0, plane - 1)], plane_sems.at[0])
+    drain(line_recv.at[pl.ds(0, n_tp - 1)], line_sems.at[0])
+    drain(seg_recv.at[pl.ds(0, plane - 1)], seg_sems.at[0])
+    drain(seg_mate, mate_sems.at[0])
+    drain(state_send, pair_sems.at[len(blocks)])
+    drain(pair_send.at[pl.ds(0, len(blocks) - 1)], state_sems.at[0])
+    if across:
+        drain(xt_recv.at[pl.ds(0, n_dp - 1)], xt_sems.at[0])
+        drain(bt_recv.at[pl.ds(0, n_dp - 1)], bt_sems.at[0])
+    drain(col_recv.at[pl.ds(0, ring - 1)], col_sems.at[0])
+    drain(sq_recv.at[pl.ds(0, ring - 1)], sq_sems.at[0])
+    drain(out_recv.at[pl.ds(0, ring - 1)], out_sems.at[0])
+
+    drain(sq_recv.at[pl.ds(0, ring - 1)], sq_sems.at[1])
     total_squares = sq_recv[0]
+    for i in range(1, ring):
+        total_squares = total_squares + sq_recv[i]
+    total_squares = jnp.sum(jnp.where(diagonal, total_squares, 0.0), axis=1, keepdims=True)
+    inverse = lax.rsqrt(total_squares / (total_heads * dim) + epsilon)
+    drain(out_recv.at[pl.ds(0, ring - 1)], out_sems.at[1])
     mixed = out_recv[0].astype(F32)
-    for i in range(1, n_ctx * n_tp):
-        total_squares = total_squares + sq_recv[i]
+    for i in range(1, ring):
         mixed = mixed + out_recv[i].astype(F32)
-    inverse = lax.rsqrt(total_squares[:, 0:1] / (total_heads * dim) + epsilon)
     mixed = mixed * inverse
     for t in range(steps):
         mixed_ref[t] = at(mixed, t).astype(BF16)
-    for copy in (
-        emb_copies + seg_copies + pair_copies + xt_copies + bt_copies + state_copies + col_copies + sq_copies
-        + out_copies
-    ):
-        copy.wait_send()
-    final_copy.wait()
-
-
-def tail_kernel(mixed_in, final_in, mixed_out, final_out, mixed_buf, final_buf, in_sems, out_sems):
-    moves = [(mixed_in, mixed_buf, mixed_out)]
-    cuts = 4 if final_in.shape[1] % 32 == 0 else 1
-    size = final_in.shape[1] // cuts
-    for j in range(final_in.shape[0]):
-        for k in range(cuts):
-            piece = (j, pl.ds(k * size, size))
-            moves.append((final_in.at[piece], final_buf.at[piece], final_out.at[piece]))
-    moves = moves[1:] + moves[:1]
-    inward = [pltpu.make_async_copy(a, b, in_sems.at[i]) for i, (a, b, _) in enumerate(moves)]
-    outward = [pltpu.make_async_copy(b, e, out_sems.at[i]) for i, (_, b, e) in enumerate(moves)]
-    for copy in inward:
-        copy.start()
-    for first, second in zip(inward, outward):
-        first.wait()
-        second.start()
-    for copy in outward:
-        copy.wait()
 
 
 def kernel_device(
@@ -696,25 +681,25 @@
     heads, dim, model = w_zx.shape[1:]
     chans = heads * dim
     tp_heads, state_n = state_parts.shape[2], state_parts.shape[4]
-    world, ring = n_ctx * n_dp * n_tp, n_ctx * n_tp
+    ring, plane, blocks = n_ctx * n_tp, n_dp * n_ctx, n_dp * (n_ctx // 2)
     smem = pl.BlockSpec(memory_space=pltpu.SMEM)
     vmem = pl.BlockSpec(memory_space=pltpu.VMEM)
     anywhere = pl.BlockSpec(memory_space=pl.ANY)
+    sem = pltpu.SemaphoreType.DMA
     rest = max(1, vocab % ROW_TILE)
     part = pl.pallas_call(
         functools.partial(gather_kernel, steps, slots, n_dp),
-        out_shape=jax.ShapeDtypeStruct((n_dp, rows, feats), BF16),
+        out_shape=pltpu.VMEM((n_dp, rows, feats), BF16),
         in_specs=[smem, smem, anywhere],
         out_specs=vmem,
         scratch_shapes=[
             pltpu.VMEM((steps * slots, ROW_TILE, feats), BF16),
             pltpu.VMEM((rest, feats), BF16),
-            pltpu.SemaphoreType.DMA((steps * slots,)),
-            pltpu.SemaphoreType.DMA,
+            sem,
+            sem,
         ],
         name="gather_rows",
     )(token_ids, decode_prompt, embedding)
-    sem = pltpu.SemaphoreType.DMA
     wide = 2 * state_n
     full_rows = -(-(conv_x_weight.shape[0] - 1 + steps) * per // 8) * 8
     smalls = (
@@ -729,35 +714,37 @@
         gate_norm_gain,
     )
     bc_planes = jnp.swapaxes(bc_tail, 0, 1)
-    outs = (
-        jax.ShapeDtypeStruct((steps, per, feats), BF16),
-        jax.ShapeDtypeStruct((per, chans, state_n), F32),
-    )
-    pairs = n_ctx // 2
     mixed, final = pl.pallas_call(
         functools.partial(mixer_kernel, sizes),
-        out_shape=outs,
-        in_specs=[smem] + [anywhere] * 17,
-        out_specs=(vmem, anywhere),
+        out_shape=(
+            pltpu.VMEM((steps, per, feats), BF16),
+            pltpu.VMEM((per, chans, state_n), F32),
+        ),
+        in_specs=[anywhere, vmem] + [anywhere] * 16,
+        out_specs=(vmem, vmem),
         scratch_shapes=[
+            pltpu.SMEM((slots,), jnp.int32),
             *[pltpu.VMEM(small.shape, small.dtype) for small in smalls],
-            pltpu.VMEM((per, chans, state_n), F32),
-            pltpu.VMEM((n_dp, pairs, chans, state_n), BF16),
-            pltpu.VMEM((n_dp, pairs, chans, state_n), BF16),
+            pltpu.VMEM((blocks, chans, state_n), BF16),
+            pltpu.VMEM((blocks, chans, state_n), BF16),
             pltpu.VMEM((2 * chans, model), BF16),
             pltpu.VMEM(w_bcdt.shape[::-1], BF16),
             pltpu.VMEM((chans, model), BF16),
             pltpu.VMEM((per, tp_heads * dim, state_n), BF16),
-            pltpu.VMEM((n_dp, tp_heads * dim, state_n), BF16),
-            pltpu.VMEM((n_dp, pairs, chans, state_n), BF16),
-            pltpu.VMEM((n_dp, ring, rows, feats), BF16),
-            pltpu.VMEM((n_dp, n_ctx, per, tp_heads), F32),
+            pltpu.VMEM((blocks, chans, state_n), BF16),
+            pltpu.VMEM((blocks, chans, state_n), BF16),
+            pltpu.VMEM((plane, rows, feats), BF16),
+            pltpu.VMEM((n_ctx, rows, feats), BF16),
+            pltpu.VMEM((n_tp, n_ctx, rows, feats), BF16),
+            pltpu.VMEM((plane, per, tp_heads), F32),
+            pltpu.VMEM((per, tp_heads), F32),
+            pltpu.VMEM((per, tp_heads), F32),
             pltpu.VMEM((n_dp,) + x_tail.shape, BF16),
             pltpu.VMEM((n_dp,) + bc_planes.shape, BF16),
             pltpu.VMEM((rows, 128), F32),
             pltpu.VMEM((ring, rows, 128), F32),
-            pltpu.VMEM((rows, 128), F32),
-            pltpu.VMEM((ring, rows, 128), F32),
+            pltpu.VMEM((1, 128), F32),
+            pltpu.VMEM((ring, 1, 128), F32),
             pltpu.VMEM((ring, rows, feats), BF16),
             pltpu.VMEM((ring, rows, feats), BF16),
             pltpu.VMEM((per, chans, state_n), F32),
@@ -766,19 +753,9 @@
             pltpu.VMEM((rows, chans), F32),
             sem((5,)),
             sem((len(smalls),)),
-            sem((5,)),
-            sem,
-            sem((2, n_dp * pairs + 1)),
-            pltpu.VMEM((per, tp_heads), F32),
-            pltpu.VMEM((per, tp_heads), F32),
-            sem((2, world)),
-            sem((2, n_dp * pairs)),
-            sem((2, n_ctx * n_dp)),
-            sem((2, n_dp)),
-            sem((2, n_dp)),
-            sem((2, ring)),
-            sem((2, ring)),
-            sem((2, ring)),
+            sem((4,)),
+            sem((blocks + 1,)),
+            *[sem((2,))] * 10,
         ],
         compiler_params=pltpu.CompilerParams(
             collective_id=0, has_side_effects=True, vmem_limit_bytes=56 * 1024 * 1024
@@ -786,7 +763,7 @@
         name="mixer",
     )(
         decode_prompt,
-        part,
+        pltpu.with_memory_space_constraint(part, pltpu.VMEM),
         seg_rate,
         x_tail,
         bc_planes,
@@ -796,19 +773,6 @@
         w_out.reshape(chans, model),
         state_parts.reshape(per, tp_heads * dim, state_n),
     )
-    mixed, final = pl.pallas_call(
-        tail_kernel,
-        out_shape=outs,
-        in_specs=[anywhere] * 2,
-        out_specs=(anywhere, anywhere),
-        scratch_shapes=[
-            pltpu.VMEM(outs[0].shape, BF16),
-            pltpu.VMEM(outs[1].shape, F32),
-            sem((4 * per + 1,)),
-            sem((4 * per + 1,)),
-        ],
-        name="tail",
-    )(mixed, final)
     return mixed, final.reshape(per, heads, dim, state_n)
 
 

time: 32.3 us -> 27.2 us (0.84)
  Pallas kernels: 31.4 us -> 24.9 us
  local copies, waits for them, and re-layouts: 0 us -> 1.39 us
    pallas_call x2 -> x1, Pallas kernels: 28.7 us -> 23.1 us  [kernel_device(): pl.pallas_call(functools.partial(mixer_kernel, sizes), out_shape=(pltpu.V...]
    unnamed x0 -> x2, local copies, waits for them, and re-layouts: none -> 1.39 us
    pallas_call x1, Pallas kernels: 2.64 us -> 1.83 us  [kernel_device(): pl.pallas_call(functools.partial(gather_kernel, steps, slots, n_dp), out_...]
where the time goes in v1:
time: 27.2 us; the launch traced here: 26.9 us
  Pallas kernels  24.9 us (92%)
  local copies, waits for them, and re-layouts  1.39 us (5%)
  between operations  0.65 us (2%)
    pallas_call x1, Pallas kernels, kernel_device(): pl.pallas_call(functools.partial(mixer_kernel, sizes), out_shape=(pltpu.V...  23.1 us
    pallas_call x1, Pallas kernels, kernel_device(): pl.pallas_call(functools.partial(gather_kernel, steps, slots, n_dp), out_...  1.83 us
    unnamed x2, local copies, waits for them, and re-layouts  1.39 us

profile of v1, /device:TPU:0, one launch (start us, length us, event | category | flops | bytes accessed | tf_op | source)
XLA Modules:
  0.0 26.9 jit_solution(6280372269552639490)
XLA Ops:
  0.6 1.8 %gather_rows.1.part_ref = bf16[2,8,256]{2,1,0:T(8,128)(2,1)S(1)} custom-call(s32[4,4]{1,0:T(4,128)} %tok_ref.1, s32[4]{0:T(128)} %dec_hbm.1, bf16[25140,256]{1,0:T(8,128)(2,1)} %emb_ref.1), custom_call_target="tpu_custom_call" | custom-call | tf_op jit(solution)/shard_map/gather_rows/pallas_call | solution.py:690
  2.5 23.1 %mixer.1 = (bf16[4,2,256]{2,1,0:T(2,128)(2,1)S(1)}, f32[2,512,128]{2,1,0:T(8,128)S(1)}) custom-call(s32[4]{0:T(128)} %dec_hbm.1, bf16[2,8,256]{2,1,0:T(8,128)(2,1)S(1)} %gather_rows.1.part_ref, f32[1,2,32]{2,1,0:T(2,128)} %seg_hbm.1, bf16[2,3,8,64]{3,2,1,0:T(8,128)(2,1)} %xt_hbm.1, bf16[3,2,256]{2,1,0:T(2,128)(2,1)} %bitcast.17, f32[1,4096]{1,0:T(1,128)} %bitcast.16, ...), custom_call_target="tpu_custom_call" | custom-call | tf_op jit(solution)/shard_map/mixer/pallas_call | solution.py:717
  25.5 0.6 %copy.23 = bf16[4,2,256]{2,1,0:T(2,128)(2,1)} copy(bf16[4,2,256]{2,1,0:T(2,128)(2,1)S(1)} %get-tuple-element.6) | data formatting | bytes 8192
  26.1 0.8 %copy.24 = f32[2,8,64,128]{3,2,1,0:T(8,128)} copy(f32[2,8,64,128]{3,2,1,0:T(8,128)S(1)} %bitcast.11) | data formatting | bytes 1048576

commit v2 on v1

--- a/solution.py
+++ b/solution.py
@@ -383,9 +383,6 @@
     fetch(*pairs[0], load_sems.at[0], loads)
     for i, pair in enumerate(small_pairs):
         fetch(*pair, small_sems.at[i], smalls)
-    for i, pair in enumerate(pairs[1:]):
-        fetch(*pair, load_sems.at[i + 1], loads)
-
     def send(source, target, send_sem, recv_sem, place):
         pltpu.make_async_remote_copy(
             src_ref=source,
@@ -414,6 +411,11 @@
     send(seg_own, seg_mate, mate_sems.at[0], mate_sems.at[1], mate)
     for o in routed:
         send(seg_own, seg_recv.at[here_plane], seg_sems.at[0], seg_sems.at[1], device(o))
+    owns[2].wait()
+    owns[3].wait()
+    for o in across:
+        send(xt_recv.at[d], xt_recv.at[d], xt_sems.at[0], xt_sems.at[1], device(o))
+        send(bt_recv.at[d], bt_recv.at[d], bt_sems.at[0], bt_sems.at[1], device(o))
     picks = []
     for b in range(n_dp):
         target_group = lax.rem(d + b, n_dp)
@@ -427,11 +429,9 @@
         first = pl.multiple_of(lax.rem(mate["ctx"] + 2 * a, n_ctx) * chans, chans)
         state_send[slot] = state_in[picks[b], pl.ds(first, chans), :]
         send(state_send.at[slot], pair_recv.at[slot], pair_sems.at[len(blocks)], pair_sems.at[slot], mate)
-    owns[2].wait()
-    owns[3].wait()
-    for o in across:
-        send(xt_recv.at[d], xt_recv.at[d], xt_sems.at[0], xt_sems.at[1], device(o))
-        send(bt_recv.at[d], bt_recv.at[d], bt_sems.at[0], bt_sems.at[1], device(o))
+
+    for i, pair in enumerate(pairs[1:]):
+        fetch(*pair, load_sems.at[i + 1], loads)
 
     fold = (
         lax.broadcasted_iota(jnp.int32, (dim, chans), 0)
@@ -451,16 +451,6 @@
             == first + lax.div(lax.broadcasted_iota(jnp.int32, (count, chans), 1), dim)
         ).astype(F32)
         return f32_dot(value, chosen)
-
-    drain(plane_recv.at[pl.ds(0, plane - 1)], plane_sems.at[1])
-    for i in range(n_ctx):
-        piece = plane_recv[i].astype(F32)
-        for g in range(1, n_dp):
-            piece += plane_recv[g * n_ctx + i].astype(F32)
-        line_send[i] = piece.astype(BF16)
-    for o in line:
-        send(line_send, line_recv.at[p], line_sems.at[0], line_sems.at[1], device(o))
-    line_recv[p] = line_send[...]
 
     drain(seg_mate, mate_sems.at[1])
     shrink = []
@@ -488,6 +478,17 @@
         else:
             state_recv[d * half_ctx + lax.div(c, 2)] = added
 
+    drain(plane_recv.at[pl.ds(0, plane - 1)], plane_sems.at[1])
+    for i in range(n_ctx):
+        piece = plane_recv[i].astype(F32)
+        for g in range(1, n_dp):
+            piece += plane_recv[g * n_ctx + i].astype(F32)
+        line_send[i] = piece.astype(BF16)
+    for o in line:
+        send(line_send, line_recv.at[p], line_sems.at[0], line_sems.at[1], device(o))
+    line_recv[p] = line_send[...]
+
+
     for load in smalls:
         load.wait()
     tap_rows = [flat(cxw_ref[k]) for k in range(taps)]
@@ -648,6 +649,17 @@
     mixed = mixed * inverse
     for t in range(steps):
         mixed_ref[t] = at(mixed, t).astype(BF16)
+
+
+def tail_kernel(mixed_in, final_in, mixed_out, final_out, sems):
+    copies = [
+        pltpu.make_async_copy(final_in, final_out, sems.at[0]),
+        pltpu.make_async_copy(mixed_in, mixed_out, sems.at[1]),
+    ]
+    for copy in copies:
+        copy.start()
+    for copy in copies:
+        copy.wait()
 
 
 def kernel_device(
@@ -773,6 +785,20 @@
         w_out.reshape(chans, model),
         state_parts.reshape(per, tp_heads * dim, state_n),
     )
+    mixed, final = pl.pallas_call(
+        tail_kernel,
+        out_shape=(
+            jax.ShapeDtypeStruct(mixed.shape, BF16),
+            jax.ShapeDtypeStruct(final.shape, F32),
+        ),
+        in_specs=[anywhere] * 2,
+        out_specs=(anywhere, anywhere),
+        scratch_shapes=[sem((2,))],
+        name="tail",
+    )(
+        pltpu.with_memory_space_constraint(mixed, pltpu.VMEM),
+        pltpu.with_memory_space_constraint(final, pltpu.VMEM),
+    )
     return mixed, final.reshape(per, heads, dim, state_n)
 
 

time: 27.2 us -> 25.9 us (0.952)
  local copies, waits for them, and re-layouts: 1.39 us -> 0 us
    unnamed x2 -> x0, local copies, waits for them, and re-layouts: 1.39 us -> none
    pallas_call x0 -> x1, Pallas kernels: none -> 0.81 us  [kernel_device(): pl.pallas_call(tail_kernel, out_shape=(jax.ShapeDtypeStruct(mixed.shape,...]
    pallas_call x1, Pallas kernels: 23.1 us -> 22.4 us  [kernel_device(): pl.pallas_call(functools.partial(mixer_kernel, sizes), out_shape=(pltpu.V...]
where the time goes in v2:
time: 25.9 us; the launch traced here: 25.7 us
  Pallas kernels  25 us (97%)
  between operations  0.65 us (3%)
    pallas_call x1, Pallas kernels, kernel_device(): pl.pallas_call(functools.partial(mixer_kernel, sizes), out_shape=(pltpu.V...  22.4 us
    pallas_call x1, Pallas kernels, kernel_device(): pl.pallas_call(functools.partial(gather_kernel, steps, slots, n_dp), out_...  1.84 us
    pallas_call x1, Pallas kernels, kernel_device(): pl.pallas_call(tail_kernel, out_shape=(jax.ShapeDtypeStruct(mixed.shape,...  0.81 us

profile of v2, /device:TPU:0, one launch (start us, length us, event | category | flops | bytes accessed | tf_op | source)
XLA Modules:
  0.0 25.7 jit_solution(3409637340788237685)
XLA Ops:
  0.6 1.8 %gather_rows.1.part_ref = bf16[2,8,256]{2,1,0:T(8,128)(2,1)S(1)} custom-call(s32[4,4]{1,0:T(4,128)} %tok_ref.1, s32[4]{0:T(128)} %dec_hbm.1, bf16[25140,256]{1,0:T(8,128)(2,1)} %emb_ref.1), custom_call_target="tpu_custom_call" | custom-call | tf_op jit(solution)/shard_map/gather_rows/pallas_call | solution.py:702
  2.5 22.4 %mixer.1 = (bf16[4,2,256]{2,1,0:T(2,128)(2,1)S(1)}, f32[2,512,128]{2,1,0:T(8,128)S(1)}) custom-call(s32[4]{0:T(128)} %dec_hbm.1, bf16[2,8,256]{2,1,0:T(8,128)(2,1)S(1)} %gather_rows.1.part_ref, f32[1,2,32]{2,1,0:T(2,128)} %seg_hbm.1, bf16[2,3,8,64]{3,2,1,0:T(8,128)(2,1)} %xt_hbm.1, bf16[3,2,256]{2,1,0:T(2,128)(2,1)} %bitcast.16, f32[1,4096]{1,0:T(1,128)} %bitcast.15, ...), custom_call_target="tpu_custom_call" | custom-call | tf_op jit(solution)/shard_map/mixer/pallas_call | solution.py:729
  24.8 0.8 %tail.1 = (bf16[4,2,256]{2,1,0:T(2,128)(2,1)}, f32[2,512,128]{2,1,0:T(8,128)}) custom-call(bf16[4,2,256]{2,1,0:T(2,128)(2,1)S(1)} %get-tuple-element.6.mixed_in, f32[2,512,128]{2,1,0:T(8,128)S(1)} %get-tuple-element.7.final_in), custom_call_target="tpu_custom_call" | custom-call | tf_op jit(solution)/shard_map/tail/pallas_call | solution.py:788

commit v3 on v2

--- a/solution.py
+++ b/solution.py
@@ -178,7 +178,7 @@
     return jnp.maximum(v, 0.0) + jnp.log1p(jnp.exp(-jnp.abs(v)))
 
 
-ROW_TILE = 16
+ROW_TILE = 8
 
 
 def drain(ref, sem):
@@ -284,23 +284,25 @@
     out_send,
     out_recv,
     start_state,
+    start_low,
     xfull,
     bcfull,
-    gated_ref,
     load_sems,
     small_sems,
     own_sems,
     pair_sems,
-    mate_sems,
-    state_sems,
-    plane_sems,
-    line_sems,
-    seg_sems,
-    xt_sems,
-    bt_sems,
-    col_sems,
-    sq_sems,
-    out_sems,
+    mate_sem,
+    state_sem,
+    plane_sem,
+    line_sem,
+    seg_sem,
+    xt_sem,
+    bt_sem,
+    col_sem,
+    sq_sem,
+    out_sem,
+    done,
+    ready,
 ):
     n_ctx, n_dp, n_tp, total_heads = sizes
     c, d, p = lax.axis_index("ctx"), lax.axis_index("dp"), lax.axis_index("tp")
@@ -332,17 +334,27 @@
         a, b, e = peer(offset)
         return {"ctx": a, "dp": b, "tp": e}
 
+    def along(k):
+        return {"ctx": c, "dp": d, "tp": lax.rem(p + k + n_tp, n_tp)}
+
     far = [1, 2, 3] if mirror else list(range(n_tp - 1, 0, -1))
     routed = [(a, b, 0) for a in reversed(range(n_ctx)) for b in reversed(range(n_dp)) if a + b]
-    line = [(0, 0, e) for e in far]
     group = [(a, 0, e) for e in far + [0] for a in reversed(range(n_ctx)) if a + e]
     across = [(0, b, 0) for b in range(1, n_dp)]
 
     barrier = pltpu.get_barrier_semaphore()
-    for o in line + routed:
+    for o in routed:
         pl.semaphore_signal(
             barrier, inc=1, device_id=device(o), device_id_type=pl.DeviceIdType.MESH
         )
+    for k in range(1, n_tp):
+
+        @pl.when(p + k < n_tp)
+        def _():
+            pl.semaphore_signal(
+                barrier, inc=1, device_id=along(k), device_id_type=pl.DeviceIdType.MESH
+            )
+
 
     owns = []
     for source, target in (
@@ -393,12 +405,18 @@
             device_id_type=pl.DeviceIdType.MESH,
         ).start()
 
-    col_send[...] = jnp.zeros_like(col_send)
-
-    pl.semaphore_wait(barrier, len(line) + len(routed))
+    pl.semaphore_wait(barrier, len(routed) + p)
+    for k in range(1, n_tp):
+
+        @pl.when(p >= k)
+        def _():
+            pl.semaphore_signal(
+                ready, inc=1, device_id=along(-k), device_id_type=pl.DeviceIdType.MESH
+            )
+
 
     for o in routed:
-        send(part_ref.at[peer(o)[1]], plane_recv.at[here_plane], plane_sems.at[0], plane_sems.at[1], device(o))
+        send(part_ref.at[peer(o)[1]], plane_recv.at[here_plane], done, plane_sem, device(o))
     plane_recv[here_plane] = part_ref[d]
 
     owns[0].wait()
@@ -408,14 +426,14 @@
     half_ctx = n_ctx // 2
     blocks = [(a, b) for a in reversed(range(half_ctx)) for b in reversed(range(n_dp))]
     seg_recv[here_plane] = seg_own[...]
-    send(seg_own, seg_mate, mate_sems.at[0], mate_sems.at[1], mate)
+    send(seg_own, seg_mate, done, mate_sem, mate)
     for o in routed:
-        send(seg_own, seg_recv.at[here_plane], seg_sems.at[0], seg_sems.at[1], device(o))
+        send(seg_own, seg_recv.at[here_plane], done, seg_sem, device(o))
     owns[2].wait()
     owns[3].wait()
     for o in across:
-        send(xt_recv.at[d], xt_recv.at[d], xt_sems.at[0], xt_sems.at[1], device(o))
-        send(bt_recv.at[d], bt_recv.at[d], bt_sems.at[0], bt_sems.at[1], device(o))
+        send(xt_recv.at[d], xt_recv.at[d], done, xt_sem, device(o))
+        send(bt_recv.at[d], bt_recv.at[d], done, bt_sem, device(o))
     picks = []
     for b in range(n_dp):
         target_group = lax.rem(d + b, n_dp)
@@ -428,7 +446,7 @@
     for slot, (a, b) in enumerate(blocks):
         first = pl.multiple_of(lax.rem(mate["ctx"] + 2 * a, n_ctx) * chans, chans)
         state_send[slot] = state_in[picks[b], pl.ds(first, chans), :]
-        send(state_send.at[slot], pair_recv.at[slot], pair_sems.at[len(blocks)], pair_sems.at[slot], mate)
+        send(state_send.at[slot], pair_recv.at[slot], done, pair_sems.at[slot], mate)
 
     for i, pair in enumerate(pairs[1:]):
         fetch(*pair, load_sems.at[i + 1], loads)
@@ -452,7 +470,7 @@
         ).astype(F32)
         return f32_dot(value, chosen)
 
-    drain(seg_mate, mate_sems.at[1])
+    drain(seg_mate, mate_sem)
     shrink = []
     for b in range(n_dp):
         row = pl.ds(picks[b], 1)
@@ -474,18 +492,32 @@
         target = state_recv.at[d * half_ctx + lax.div(c, 2)]
         if a + b:
             pair_send[slot] = added
-            send(pair_send.at[slot], target, state_sems.at[0], state_sems.at[1], device((2 * a, b, 0)))
+            send(pair_send.at[slot], target, done, state_sem, device((2 * a, b, 0)))
         else:
             state_recv[d * half_ctx + lax.div(c, 2)] = added
 
-    drain(plane_recv.at[pl.ds(0, plane - 1)], plane_sems.at[1])
+    drain(plane_recv.at[pl.ds(0, plane - 1)], plane_sem)
     for i in range(n_ctx):
         piece = plane_recv[i].astype(F32)
         for g in range(1, n_dp):
             piece += plane_recv[g * n_ctx + i].astype(F32)
         line_send[i] = piece.astype(BF16)
-    for o in line:
-        send(line_send, line_recv.at[p], line_sems.at[0], line_sems.at[1], device(o))
+    for k in range(n_tp - 1, 0, -1):
+
+        @pl.when(p >= k)
+        def _():
+            send(line_send, line_recv.at[p], done, line_sem, along(-k))
+
+    @pl.when(p < n_tp - 1)
+    def _():
+        pl.semaphore_wait(ready, n_tp - 1 - p)
+
+    for k in range(n_tp - 1, 0, -1):
+
+        @pl.when(p + k < n_tp)
+        def _():
+            send(line_send, line_recv.at[p], done, line_sem, along(k))
+
     line_recv[p] = line_send[...]
 
 
@@ -494,15 +526,16 @@
     tap_rows = [flat(cxw_ref[k]) for k in range(taps)]
     bias_row = flat(cxb_ref[...])
     gate_row = flat(gg_ref[...])
-    dtb_row = spread(dtb_ref[...], 0)
-    rate_row = -jnp.exp(spread(alog_ref[...], 0))
-    skip_row = spread(skip_ref[...], 0)
+    idle = jnp.zeros((1, total_heads - heads), F32)
+    dtb_row = jnp.concatenate([dtb_ref[...], idle], axis=1)
+    rate_row = jnp.concatenate([-jnp.exp(alog_ref[...]), idle], axis=1)
+    skip_row = jnp.concatenate([skip_ref[...], idle], axis=1)
 
     holders = [lax.div(dec_ref[d * per + j], per) for j in range(per)]
     places = [lax.rem(dec_ref[d * per + j], per) for j in range(per)]
-    for sems, ref in ((xt_sems, xt_recv), (bt_sems, bt_recv)):
+    for one, ref in ((xt_sem, xt_recv), (bt_sem, bt_recv)):
         if across:
-            drain(ref.at[pl.ds(0, n_dp - 1)], sems.at[1])
+            drain(ref.at[pl.ds(0, n_dp - 1)], one)
     plane_rows = lax.broadcasted_iota(jnp.int32, (per, 1), 0)
     for k in range(taps - 1):
         for j in range(per):
@@ -513,7 +546,7 @@
                 jnp.where(plane_rows == places[j], tail, 0.0), axis=0, keepdims=True
             )
 
-    drain(seg_recv.at[pl.ds(0, plane - 1)], seg_sems.at[1])
+    drain(seg_recv.at[pl.ds(0, plane - 1)], seg_sem)
     weights = []
     for j in range(per):
         after = jnp.zeros((1, tp_heads), F32)
@@ -526,20 +559,22 @@
         weights.extend(reversed(ordered))
     weight_cols = jnp.transpose(spread(jnp.concatenate(weights, axis=0), c * heads))
 
-    drain(line_recv.at[pl.ds(0, n_tp - 1)], line_sems.at[1])
+    drain(line_recv.at[pl.ds(0, n_tp - 1)], line_sem)
     pieces = [line_recv[e, i].astype(F32) for i in range(n_ctx) for e in range(n_tp)]
     embedded = jnp.concatenate(pieces, axis=1)
     scale = lax.rsqrt(jnp.sum(embedded * embedded, axis=1, keepdims=True) / model + epsilon)
-    normed = (embedded * scale * gain_ref[...]).astype(BF16)
+    normed = (embedded * gain_ref[...]).astype(BF16)
     loads[1].wait()
-    col_send[:, 0:n_cols] = nt_dot(normed, wbc[...])
+    narrow = nt_dot(normed, wbc[...]) * scale
+    padded = jnp.concatenate([narrow, jnp.zeros((rows, 128 - n_cols), F32)], axis=1)
+    col_send[...] = pltpu.roll(padded, lax.rem(n_cols * mine, 128), 1)
     for o in group:
-        send(col_send, col_recv.at[mine], col_sems.at[0], col_sems.at[1], device(o))
+        send(col_send, col_recv.at[mine], done, col_sem, device(o))
     col_recv[mine] = col_send[...]
     loads[2].wait()
-    x_rows = nt_dot(normed, wzx[half : 2 * half, :])
+    x_rows = nt_dot(normed, wzx[half : 2 * half, :]) * scale
     loads[3].wait()
-    z_gate = silu(nt_dot(normed, wzx[0:half, :]))
+    z_gate = silu(nt_dot(normed, wzx[0:half, :]) * scale)
 
     lead = (taps - 1) * per
     xfull[lead : lead + rows, :] = x_rows
@@ -548,7 +583,7 @@
         conv = conv + tap_rows[k] * xfull[k * per : k * per + rows, :]
     xc = silu(conv)
 
-    drain(state_recv.at[pl.ds(0, n_dp * half_ctx - 1)], state_sems.at[1])
+    drain(state_recv.at[pl.ds(0, n_dp * half_ctx - 1)], state_sem)
     for j in range(per):
         begin = None
         for m in range(half_ctx):
@@ -556,66 +591,102 @@
             term = weight_cols[:, r : r + 1] * state_recv[holders[j] * half_ctx + m].astype(F32)
             begin = term if begin is None else begin + term
         start_state[j] = begin
-
-    drain(col_recv.at[pl.ds(0, ring - 1)], col_sems.at[1])
-    wide_pad = jnp.zeros((rows, all_cols - col_send.shape[1]), F32)
-    columns = jnp.zeros((rows, all_cols), F32)
-    for i in range(ring):
-        wide = jnp.concatenate([col_recv[i], wide_pad], axis=1)
-        columns = columns + (pltpu.roll(wide, n_cols * i, 1) if i else wide)
+        start_low[j] = begin.astype(BF16)
+
+    drain(col_recv.at[pl.ds(0, ring - 1)], col_sem)
+    lanes = lax.broadcasted_iota(jnp.int32, (rows, 128), 1)
+    blocks_of = []
+    for v in range(-(-all_cols // 128)):
+        block = jnp.zeros((rows, 128), F32)
+        for i in range(ring):
+            low = n_cols * i - 128 * v
+            if low < 128 and low + n_cols > 0:
+                block = jnp.where((lanes >= low) & (lanes < low + n_cols), col_recv[i], block)
+        blocks_of.append(block)
+    columns = jnp.concatenate(blocks_of, axis=1)
     bcfull[lead : lead + rows, :] = columns[:, :width]
+    head_first = (p * n_ctx + c) * heads
+    dt_raw = pltpu.roll(columns[:, width:all_cols], total_heads - head_first, 1)
+    step_size = softplus(dt_raw + dtb_row)
+    row_of = lax.broadcasted_iota(jnp.int32, (rows, 1), 0)
+
+    def later(value, k):
+        return pltpu.roll(value, k * per, 0) if k else value
+
+    total = step_size * rate_row
+    k = 1
+    while k < steps:
+        total = total + jnp.where(row_of >= k * per, later(total, k), 0.0)
+        k *= 2
     conv = cbb_ref[...]
     for k in range(taps):
         conv = conv + cbw_ref[k : k + 1, :] * bcfull[k * per : k * per + rows, :]
     bcc = silu(conv)
     b_all, c_all = bcc[:, :state_n], bcc[:, state_n:]
-    head_first = (p * n_ctx + c) * heads
-    step_size = softplus(spread(columns[:, width:], head_first) + dtb_row)
-    log_keep = step_size * rate_row
-    driven = step_size * xc
-
-    row_slot = lax.rem(lax.broadcasted_iota(jnp.int32, (rows, 1), 0), per)
+
+    row_slot = lax.rem(row_of, per)
     from_start = jnp.zeros((rows, chans), F32)
     c_low = c_all.astype(BF16)
     for j in range(per):
-        from_start += jnp.where(row_slot == j, nt_dot(c_low, start_state[j].astype(BF16)), 0.0)
+        from_start += jnp.where(row_slot == j, nt_dot(c_low, start_low[j]), 0.0)
+
+    def by_head(value):
+        if 128 % dim or chans % 128:
+            return spread(value, 0)
+        packed = 128 // dim
+        out = []
+        for m in range(chans // 128):
+            part = jnp.broadcast_to(value[:, m * packed : m * packed + 1], (rows, 128))
+            for q in range(1, packed):
+                one = value[:, m * packed + q : m * packed + q + 1]
+                part = jnp.where(lanes >= q * dim, one, part)
+            out.append(part)
+        return jnp.concatenate(out, axis=1)
 
     def at(value, t):
         return value[t * per : (t + 1) * per]
 
-    total = jnp.zeros((per, chans), F32)
-    sums = []
-    for t in range(steps):
-        total = total + at(log_keep, t)
-        sums.append(total)
-    for t in range(steps):
-        y = jnp.exp(sums[t]) * at(from_start, t) + skip_row * at(xc, t)
-        for s in range(t + 1):
-            overlap = jnp.sum(at(b_all, s) * at(c_all, t), axis=1, keepdims=True)
-            term = at(driven, s) * overlap
-            y = y + (term if s == t else jnp.exp(sums[t] - sums[s]) * term)
-        gated_ref[t * per : (t + 1) * per, :] = y
-    gated = gated_ref[...] * z_gate
-    squares = jnp.sum(gated * gated, axis=1, keepdims=True)
+    y = by_head(jnp.exp(total)) * from_start
+    for k in range(steps):
+        overlap = jnp.sum(later(b_all, k) * c_all, axis=1, keepdims=True)
+        if k:
+            valid = row_of >= k * per
+            decay = jnp.exp(jnp.where(valid, total - later(total, k), 0.0))
+            share = jnp.where(valid, decay * overlap * later(step_size, k), 0.0)
+        else:
+            share = step_size * overlap + skip_row
+        y = y + by_head(share) * later(xc, k)
+    gated = y * z_gate
     diagonal = lax.broadcasted_iota(jnp.int32, (rows, 128), 0) == lax.broadcasted_iota(
         jnp.int32, (rows, 128), 1
     )
-    sq_send[...] = jnp.sum(jnp.where(diagonal, squares, 0.0), axis=0, keepdims=True)
-    for o in group:
-        send(sq_send, sq_recv.at[mine], sq_sems.at[0], sq_sems.at[1], device(o))
-    sq_recv[mine] = sq_send[...]
-
     loads[4].wait()
-    partial = jnp.dot((gated * gate_row).astype(BF16), wout[...], preferred_element_type=F32)
-    for i in range(ring):
-        out_send[i] = partial[:, i * feats : (i + 1) * feats].astype(BF16)
-    for o in group:
-        pc, _, pp = peer(o)
-        send(out_send.at[pc * n_tp + pp], out_recv.at[mine], out_sems.at[0], out_sems.at[1], device(o))
-    out_recv[mine] = out_send[mine]
-
-    late = [jnp.exp(sums[-1] - sums[t]) * at(driven, t) for t in range(steps)]
-    flat_rows = jnp.concatenate(late + [jnp.exp(sums[-1])] * (rows // per), axis=0)
+    scaled = (gated * gate_row).astype(BF16)
+    for e in far + [0]:
+        there = peer((0, 0, e))[2]
+        cuts = [
+            wout[:, pl.ds(pl.multiple_of((a * n_tp + there) * feats, feats), feats)]
+            for a in range(n_ctx)
+        ]
+        partial = jnp.dot(scaled, jnp.concatenate(cuts, axis=1), preferred_element_type=F32)
+        for a in range(n_ctx):
+            out_send[e * n_ctx + a] = partial[:, a * feats : (a + 1) * feats].astype(BF16)
+        for a in reversed(range(n_ctx)):
+            if a + e:
+                o = (a, 0, e)
+                spot = e * n_ctx + peer(o)[0]
+                send(out_send.at[spot], out_recv.at[mine], done, out_sem, device(o))
+        if e == far[0]:
+            squares = jnp.sum(gated * gated, axis=1, keepdims=True)
+            sq_send[...] = jnp.sum(jnp.where(diagonal, squares, 0.0), axis=0, keepdims=True)
+            for o in group:
+                send(sq_send, sq_recv.at[mine], done, sq_sem, device(o))
+            sq_recv[mine] = sq_send[...]
+    out_recv[mine] = out_send[c]
+
+    last = jnp.concatenate([at(total, steps - 1)] * steps, axis=0)
+    late = by_head(jnp.exp(last - total) * step_size) * xc
+    flat_rows = jnp.concatenate([late, by_head(jnp.exp(last))], axis=0)
     tall = jnp.transpose(flat_rows)
     for j in range(per):
         b_own = jnp.where(row_slot == j, b_all, 0.0)
@@ -623,26 +694,26 @@
             tall[:, rows + j : rows + j + 1] * start_state[j] + f32_dot(tall[:, :rows], b_own)
         )
 
-    drain(plane_recv.at[pl.ds(0, plane - 1)], plane_sems.at[0])
-    drain(line_recv.at[pl.ds(0, n_tp - 1)], line_sems.at[0])
-    drain(seg_recv.at[pl.ds(0, plane - 1)], seg_sems.at[0])
-    drain(seg_mate, mate_sems.at[0])
-    drain(state_send, pair_sems.at[len(blocks)])
-    drain(pair_send.at[pl.ds(0, len(blocks) - 1)], state_sems.at[0])
+    drain(plane_recv.at[pl.ds(0, plane - 1)], done)
+    drain(line_recv.at[pl.ds(0, n_tp - 1)], done)
+    drain(seg_recv.at[pl.ds(0, plane - 1)], done)
+    drain(seg_mate, done)
+    drain(state_send, done)
+    drain(pair_send.at[pl.ds(0, len(blocks) - 1)], done)
     if across:
-        drain(xt_recv.at[pl.ds(0, n_dp - 1)], xt_sems.at[0])
-        drain(bt_recv.at[pl.ds(0, n_dp - 1)], bt_sems.at[0])
-    drain(col_recv.at[pl.ds(0, ring - 1)], col_sems.at[0])
-    drain(sq_recv.at[pl.ds(0, ring - 1)], sq_sems.at[0])
-    drain(out_recv.at[pl.ds(0, ring - 1)], out_sems.at[0])
-
-    drain(sq_recv.at[pl.ds(0, ring - 1)], sq_sems.at[1])
+        drain(xt_recv.at[pl.ds(0, n_dp - 1)], done)
+        drain(bt_recv.at[pl.ds(0, n_dp - 1)], done)
+    drain(col_recv.at[pl.ds(0, ring - 1)], done)
+    drain(sq_recv.at[pl.ds(0, ring - 1)], done)
+    drain(out_recv.at[pl.ds(0, ring - 1)], done)
+
+    drain(sq_recv.at[pl.ds(0, ring - 1)], sq_sem)
     total_squares = sq_recv[0]
     for i in range(1, ring):
         total_squares = total_squares + sq_recv[i]
     total_squares = jnp.sum(jnp.where(diagonal, total_squares, 0.0), axis=1, keepdims=True)
     inverse = lax.rsqrt(total_squares / (total_heads * dim) + epsilon)
-    drain(out_recv.at[pl.ds(0, ring - 1)], out_sems.at[1])
+    drain(out_recv.at[pl.ds(0, ring - 1)], out_sem)
     mixed = out_recv[0].astype(F32)
     for i in range(1, ring):
         mixed = mixed + out_recv[i].astype(F32)
@@ -653,9 +724,10 @@
 
 def tail_kernel(mixed_in, final_in, mixed_out, final_out, sems):
     copies = [
-        pltpu.make_async_copy(final_in, final_out, sems.at[0]),
-        pltpu.make_async_copy(mixed_in, mixed_out, sems.at[1]),
+        pltpu.make_async_copy(final_in.at[j], final_out.at[j], sems.at[j])
+        for j in range(final_in.shape[0])
     ]
+    copies.append(pltpu.make_async_copy(mixed_in, mixed_out, sems.at[len(copies)]))
     for copy in copies:
         copy.start()
     for copy in copies:
@@ -760,14 +832,15 @@
             pltpu.VMEM((ring, rows, feats), BF16),
             pltpu.VMEM((ring, rows, feats), BF16),
             pltpu.VMEM((per, chans, state_n), F32),
+            pltpu.VMEM((per, chans, state_n), BF16),
             pltpu.VMEM((full_rows, chans), F32),
             pltpu.VMEM((full_rows, wide), F32),
-            pltpu.VMEM((rows, chans), F32),
             sem((5,)),
             sem((len(smalls),)),
             sem((4,)),
-            sem((blocks + 1,)),
-            *[sem((2,))] * 10,
+            sem((blocks,)),
+            *[sem] * 11,
+            pltpu.SemaphoreType.REGULAR,
         ],
         compiler_params=pltpu.CompilerParams(
             collective_id=0, has_side_effects=True, vmem_limit_bytes=56 * 1024 * 1024
@@ -793,7 +866,7 @@
         ),
         in_specs=[anywhere] * 2,
         out_specs=(anywhere, anywhere),
-        scratch_shapes=[sem((2,))],
+        scratch_shapes=[sem((per + 1,))],
         name="tail",
     )(
         pltpu.with_memory_space_constraint(mixed, pltpu.VMEM),

time: 25.9 us -> 24.8 us (0.958)
  Pallas kernels: 25 us -> 23.9 us
    pallas_call x1, Pallas kernels: 22.4 us -> 21.2 us  [kernel_device(): pl.pallas_call(functools.partial(mixer_kernel, sizes), out_shape=(pltpu.V...]
where the time goes in v3:
time: 24.8 us; the launch traced here: 24.5 us
  Pallas kernels  23.9 us (96%)
  between operations  0.65 us (3%)
    pallas_call x1, Pallas kernels, kernel_device(): pl.pallas_call(functools.partial(mixer_kernel, sizes), out_shape=(pltpu.V...  21.2 us
    pallas_call x1, Pallas kernels, kernel_device(): pl.pallas_call(functools.partial(gather_kernel, steps, slots, n_dp), out_...  1.88 us
    pallas_call x1, Pallas kernels, kernel_device(): pl.pallas_call(tail_kernel, out_shape=(jax.ShapeDtypeStruct(mixed.shape,...  0.82 us

profile of v3, /device:TPU:0, one launch (start us, length us, event | category | flops | bytes accessed | tf_op | source)
XLA Modules:
  0.0 24.5 jit_solution(17857070653213942290)
XLA Ops:
  0.6 1.9 %gather_rows.1.part_ref = bf16[2,8,256]{2,1,0:T(8,128)(2,1)S(1)} custom-call(s32[4,4]{1,0:T(4,128)} %tok_ref.1, s32[4]{0:T(128)} %dec_hbm.1, bf16[25140,256]{1,0:T(8,128)(2,1)} %emb_ref.1), custom_call_target="tpu_custom_call" | custom-call | tf_op jit(solution)/shard_map/gather_rows/pallas_call | solution.py:774
  2.5 21.2 %mixer.1 = (bf16[4,2,256]{2,1,0:T(2,128)(2,1)S(1)}, f32[2,512,128]{2,1,0:T(8,128)S(1)}) custom-call(s32[4]{0:T(128)} %dec_hbm.1, bf16[2,8,256]{2,1,0:T(8,128)(2,1)S(1)} %gather_rows.1.part_ref, f32[1,2,32]{2,1,0:T(2,128)} %seg_hbm.1, bf16[2,3,8,64]{3,2,1,0:T(8,128)(2,1)} %xt_hbm.1, bf16[3,2,256]{2,1,0:T(2,128)(2,1)} %bitcast.16, f32[1,4096]{1,0:T(1,128)} %bitcast.15, ...), custom_call_target="tpu_custom_call" | custom-call | tf_op jit(solution)/shard_map/mixer/pallas_call | solution.py:801
  23.7 0.8 %tail.1 = (bf16[4,2,256]{2,1,0:T(2,128)(2,1)}, f32[2,512,128]{2,1,0:T(8,128)}) custom-call(bf16[4,2,256]{2,1,0:T(2,128)(2,1)S(1)} %get-tuple-element.6.mixed_in, f32[2,512,128]{2,1,0:T(8,128)S(1)} %get-tuple-element.7.final_in), custom_call_target="tpu_custom_call" | custom-call | tf_op jit(solution)/shard_map/tail/pallas_call | solution.py:861

commit v4 on v3

--- a/solution.py
+++ b/solution.py
@@ -190,35 +190,58 @@
     whole = vocab // ROW_TILE * ROW_TILE
     base = lax.axis_index("dp") * vocab
     per_group = slots // groups
-    tail_copy = None
-    if whole < vocab:
-        tail_copy = pltpu.make_async_copy(emb_ref.at[pl.ds(whole, vocab - whole)], tail, tail_sem)
-        tail_copy.start()
     where = []
+
+    def block(i, start):
+        return pltpu.make_async_copy(emb_ref.at[pl.ds(start, ROW_TILE)], buf.at[i], sem)
+
+    def rest():
+        return pltpu.make_async_copy(emb_ref.at[pl.ds(whole, vocab - whole)], tail, tail_sem)
+
+    in_tail = False
     for s in range(slots):
         q = dec_ref[s]
         for t in range(steps):
             row = tok_ref[t, q] - base
-            clipped = jnp.clip(row, 0, vocab - 1)
-            start = jnp.minimum(clipped // ROW_TILE * ROW_TILE, whole - ROW_TILE)
-            start = pl.multiple_of(start, ROW_TILE)
+            held = (row >= 0) & (row < whole)
+            start = pl.multiple_of(jnp.where(held, row, 0) // ROW_TILE * ROW_TILE, ROW_TILE)
             i = s * steps + t
-            pltpu.make_async_copy(emb_ref.at[pl.ds(start, ROW_TILE)], buf.at[i], sem).start()
-            where.append((row, start))
-    if tail_copy is not None:
-        tail_copy.wait()
-    drain(buf, sem)
+
+            @pl.when(held)
+            def _():
+                block(i, start).start()
+
+            where.append((row, start, held))
+            in_tail |= (row >= whole) & (row < vocab)
+    if whole < vocab:
+
+        @pl.when(in_tail)
+        def _():
+            rest().start()
+
+    for i, (row, start, held) in enumerate(where):
+
+        @pl.when(held)
+        def _():
+            block(i, start).wait()
+
+    if whole < vocab:
+
+        @pl.when(in_tail)
+        def _():
+            rest().wait()
+
     rows = lax.broadcasted_iota(jnp.int32, (ROW_TILE, 1), 0)
     for g in range(groups):
         picked = []
         for t in range(steps):
             for j in range(per_group):
                 i = (g * per_group + j) * steps + t
-                row, start = where[i]
+                row, start, held = where[i]
                 value = jnp.sum(
-                    jnp.where(rows == row - start, buf[i].astype(F32), 0.0), axis=0, keepdims=True
+                    jnp.where(held & (rows == row - start), buf[i].astype(F32), 0.0), axis=0, keepdims=True
                 )
-                if tail_copy is not None:
+                if whole < vocab:
                     trows = lax.broadcasted_iota(jnp.int32, (vocab - whole, 1), 0)
                     value += jnp.sum(
                         jnp.where(trows == row - whole, tail[...].astype(F32), 0.0),
@@ -285,16 +308,17 @@
     out_recv,
     start_state,
     start_low,
+    normed_ref,
     xfull,
     bcfull,
     load_sems,
-    small_sems,
+    small_sem,
     own_sems,
     pair_sems,
     mate_sem,
     state_sem,
     plane_sem,
-    line_sem,
+    line_sems,
     seg_sem,
     xt_sem,
     bt_sem,
@@ -363,7 +387,7 @@
         (xt_hbm, xt_recv.at[d]),
         (bt_hbm, bt_recv.at[d]),
     ):
-        load = pltpu.make_async_copy(source, target, own_sems.at[len(owns)])
+        load = pltpu.make_async_copy(source, target, own_sems.at[len(owns) // 2])
         load.start()
         owns.append(load)
     loads = []
@@ -393,8 +417,8 @@
         into.append(load)
 
     fetch(*pairs[0], load_sems.at[0], loads)
-    for i, pair in enumerate(small_pairs):
-        fetch(*pair, small_sems.at[i], smalls)
+    for pair in small_pairs:
+        fetch(*pair, small_sem, smalls)
     def send(source, target, send_sem, recv_sem, place):
         pltpu.make_async_remote_copy(
             src_ref=source,
@@ -506,7 +530,7 @@
 
         @pl.when(p >= k)
         def _():
-            send(line_send, line_recv.at[p], done, line_sem, along(-k))
+            send(line_send, line_recv.at[p], done, line_sems.at[p], along(-k))
 
     @pl.when(p < n_tp - 1)
     def _():
@@ -516,13 +540,29 @@
 
         @pl.when(p + k < n_tp)
         def _():
-            send(line_send, line_recv.at[p], done, line_sem, along(k))
-
-    line_recv[p] = line_send[...]
+            send(line_send, line_recv.at[p], done, line_sems.at[p], along(k))
+
+    loads[1].wait()
+    tallies = []
+
+    def take(values, e):
+        spots = [pl.ds(pl.multiple_of((i * n_tp + e) * feats, feats), feats) for i in range(n_ctx)]
+        held = jnp.concatenate([values[i].astype(F32) for i in range(n_ctx)], axis=1)
+        gains = jnp.concatenate([gain_ref[:, spot] for spot in spots], axis=1)
+        low = (held * gains).astype(BF16)
+        weights = jnp.concatenate([wbc[:, spot] for spot in spots], axis=1)
+        for i, spot in enumerate(spots):
+            normed_ref[:, spot] = low[:, i * feats : (i + 1) * feats]
+        square = held * held
+        while square.shape[1] % 256 == 0:
+            width = square.shape[1] // 2
+            square = square[:, :width] + square[:, width:]
+        tallies.append((square, nt_dot(low, weights)))
 
 
     for load in smalls:
         load.wait()
+    take([line_send[i] for i in range(n_ctx)], p)
     tap_rows = [flat(cxw_ref[k]) for k in range(taps)]
     bias_row = flat(cxb_ref[...])
     gate_row = flat(gg_ref[...])
@@ -559,22 +599,23 @@
         weights.extend(reversed(ordered))
     weight_cols = jnp.transpose(spread(jnp.concatenate(weights, axis=0), c * heads))
 
-    drain(line_recv.at[pl.ds(0, n_tp - 1)], line_sem)
-    pieces = [line_recv[e, i].astype(F32) for i in range(n_ctx) for e in range(n_tp)]
-    embedded = jnp.concatenate(pieces, axis=1)
-    scale = lax.rsqrt(jnp.sum(embedded * embedded, axis=1, keepdims=True) / model + epsilon)
-    normed = (embedded * gain_ref[...]).astype(BF16)
-    loads[1].wait()
-    narrow = nt_dot(normed, wbc[...]) * scale
-    padded = jnp.concatenate([narrow, jnp.zeros((rows, 128 - n_cols), F32)], axis=1)
+    for e in reversed(far):
+        there = peer((0, 0, e))[2]
+        drain(line_recv.at[there], line_sems.at[there])
+        take([line_recv[there, i] for i in range(n_ctx)], there)
+    square, narrow = tallies[0]
+    for more, columns in tallies[1:]:
+        square, narrow = square + more, narrow + columns
+    scale = lax.rsqrt(jnp.sum(square, axis=1, keepdims=True) / model + epsilon)
+    padded = jnp.concatenate([narrow * scale, jnp.zeros((rows, 128 - n_cols), F32)], axis=1)
     col_send[...] = pltpu.roll(padded, lax.rem(n_cols * mine, 128), 1)
     for o in group:
         send(col_send, col_recv.at[mine], done, col_sem, device(o))
     col_recv[mine] = col_send[...]
     loads[2].wait()
-    x_rows = nt_dot(normed, wzx[half : 2 * half, :]) * scale
+    x_rows = nt_dot(normed_ref[...], wzx[half : 2 * half, :]) * scale
     loads[3].wait()
-    z_gate = silu(nt_dot(normed, wzx[0:half, :]) * scale)
+    z_gate = silu(nt_dot(normed_ref[...], wzx[0:half, :]) * scale)
 
     lead = (taps - 1) * per
     xfull[lead : lead + rows, :] = x_rows
@@ -833,13 +874,16 @@
             pltpu.VMEM((ring, rows, feats), BF16),
             pltpu.VMEM((per, chans, state_n), F32),
             pltpu.VMEM((per, chans, state_n), BF16),
+            pltpu.VMEM((rows, model), BF16),
             pltpu.VMEM((full_rows, chans), F32),
             pltpu.VMEM((full_rows, wide), F32),
             sem((5,)),
-            sem((len(smalls),)),
-            sem((4,)),
+            sem,
+            sem((2,)),
             sem((blocks,)),
-            *[sem] * 11,
+            *[sem] * 3,
+            sem((n_tp,)),
+            *[sem] * 7,
             pltpu.SemaphoreType.REGULAR,
         ],
         compiler_params=pltpu.CompilerParams(

time: 24.8 us -> 24.4 us (0.984)
  Pallas kernels: 23.9 us -> 23.6 us
where the time goes in v4:
time: 24.4 us; the launch traced here: 24.2 us
  Pallas kernels  23.6 us (97%)
  between operations  0.65 us (3%)
    pallas_call x1, Pallas kernels, kernel_device(): pl.pallas_call(functools.partial(mixer_kernel, sizes), out_shape=(pltpu.V...  21 us
    pallas_call x1, Pallas kernels, kernel_device(): pl.pallas_call(functools.partial(gather_kernel, steps, slots, n_dp), out_...  1.76 us
    pallas_call x1, Pallas kernels, kernel_device(): pl.pallas_call(tail_kernel, out_shape=(jax.ShapeDtypeStruct(mixed.shape,...  0.82 us

profile of v4, /device:TPU:0, one launch (start us, length us, event | category | flops | bytes accessed | tf_op | source)
XLA Modules:
  0.0 24.2 jit_solution(9404460212086951710)
XLA Ops:
  0.6 1.8 %gather_rows.1.part_ref = bf16[2,8,256]{2,1,0:T(8,128)(2,1)S(1)} custom-call(s32[4,4]{1,0:T(4,128)} %tok_ref.1, s32[4]{0:T(128)} %dec_hbm.1, bf16[25140,256]{1,0:T(8,128)(2,1)} %emb_ref.1), custom_call_target="tpu_custom_call" | custom-call | tf_op jit(solution)/shard_map/gather_rows/pallas_call | solution.py:815
  2.4 21.0 %mixer.1 = (bf16[4,2,256]{2,1,0:T(2,128)(2,1)S(1)}, f32[2,512,128]{2,1,0:T(8,128)S(1)}) custom-call(s32[4]{0:T(128)} %dec_hbm.1, bf16[2,8,256]{2,1,0:T(8,128)(2,1)S(1)} %gather_rows.1.part_ref, f32[1,2,32]{2,1,0:T(2,128)} %seg_hbm.1, bf16[2,3,8,64]{3,2,1,0:T(8,128)(2,1)} %xt_hbm.1, bf16[3,2,256]{2,1,0:T(2,128)(2,1)} %bitcast.16, f32[1,4096]{1,0:T(1,128)} %bitcast.15, ...), custom_call_target="tpu_custom_call" | custom-call | tf_op jit(solution)/shard_map/mixer/pallas_call | solution.py:842
  23.4 0.8 %tail.1 = (bf16[4,2,256]{2,1,0:T(2,128)(2,1)}, f32[2,512,128]{2,1,0:T(8,128)}) custom-call(bf16[4,2,256]{2,1,0:T(2,128)(2,1)S(1)} %get-tuple-element.6.mixed_in, f32[2,512,128]{2,1,0:T(8,128)S(1)} %get-tuple-element.7.final_in), custom_call_target="tpu_custom_call" | custom-call | tf_op jit(solution)/shard_map/tail/pallas_call | solution.py:905

commit v5 on v4

--- a/solution.py
+++ b/solution.py
@@ -185,11 +185,19 @@
     pltpu.make_async_copy(ref, ref, sem).wait()
 
 
-def gather_kernel(steps, slots, groups, tok_ref, dec_ref, emb_ref, out_ref, buf, tail, sem, tail_sem):
+def row_place(steps, tok_ref, dec_ref, vocab, s, t):
+    whole = vocab // ROW_TILE * ROW_TILE
+    row = tok_ref[t, dec_ref[s]] - lax.axis_index("dp") * vocab
+    held = (row >= 0) & (row < whole)
+    start = pl.multiple_of(jnp.where(held, row, 0) // ROW_TILE * ROW_TILE, ROW_TILE)
+    return row, held, start
+
+
+def gather_kernel(
+    steps, slots, tok_ref, dec_ref, emb_ref, buf, tail, mark, tail_mark, sem, tail_sem
+):
     vocab = emb_ref.shape[0]
     whole = vocab // ROW_TILE * ROW_TILE
-    base = lax.axis_index("dp") * vocab
-    per_group = slots // groups
     where = []
 
     def block(i, start):
@@ -200,11 +208,8 @@
 
     in_tail = False
     for s in range(slots):
-        q = dec_ref[s]
         for t in range(steps):
-            row = tok_ref[t, q] - base
-            held = (row >= 0) & (row < whole)
-            start = pl.multiple_of(jnp.where(held, row, 0) // ROW_TILE * ROW_TILE, ROW_TILE)
+            row, held, start = row_place(steps, tok_ref, dec_ref, vocab, s, t)
             i = s * steps + t
 
             @pl.when(held)
@@ -219,6 +224,12 @@
         def _():
             rest().start()
 
+    tile_rows = lax.broadcasted_iota(jnp.int32, mark.shape[1:], 0)
+    tail_rows = whole + lax.broadcasted_iota(jnp.int32, tail_mark.shape[1:], 0)
+    for i, (row, start, held) in enumerate(where):
+        mark[i] = (held & (tile_rows == row - start)).astype(F32)
+        tail_mark[i] = (tail_rows == jnp.where(row < vocab, row, -1)).astype(F32)
+
     for i, (row, start, held) in enumerate(where):
 
         @pl.when(held)
@@ -231,31 +242,15 @@
         def _():
             rest().wait()
 
-    rows = lax.broadcasted_iota(jnp.int32, (ROW_TILE, 1), 0)
-    for g in range(groups):
-        picked = []
-        for t in range(steps):
-            for j in range(per_group):
-                i = (g * per_group + j) * steps + t
-                row, start, held = where[i]
-                value = jnp.sum(
-                    jnp.where(held & (rows == row - start), buf[i].astype(F32), 0.0), axis=0, keepdims=True
-                )
-                if whole < vocab:
-                    trows = lax.broadcasted_iota(jnp.int32, (vocab - whole, 1), 0)
-                    value += jnp.sum(
-                        jnp.where(trows == row - whole, tail[...].astype(F32), 0.0),
-                        axis=0,
-                        keepdims=True,
-                    )
-                picked.append(value)
-        out_ref[g] = jnp.concatenate(picked, axis=0).astype(BF16)
-
 
 def mixer_kernel(
     sizes,
+    vocab,
     dec_hbm,
-    part_ref,
+    raw_ref,
+    rest_ref,
+    mark_ref,
+    rest_mark_ref,
     seg_hbm,
     xt_hbm,
     bt_hbm,
@@ -275,6 +270,7 @@
     mixed_ref,
     final_ref,
     dec_ref,
+    part_ref,
     gain_ref,
     cxw_ref,
     cxb_ref,
@@ -292,9 +288,8 @@
     state_in,
     state_send,
     state_recv,
-    plane_recv,
+    rows_recv,
     line_send,
-    line_recv,
     seg_recv,
     seg_mate,
     seg_own,
@@ -361,24 +356,34 @@
     def along(k):
         return {"ctx": c, "dp": d, "tp": lax.rem(p + k + n_tp, n_tp)}
 
+    def whole_plane(k):
+        return [
+            {"ctx": a, "dp": b, "tp": lax.rem(p + k + n_tp, n_tp)}
+            for a, b, _ in [peer((a, b, 0)) for a in reversed(range(n_ctx)) for b in reversed(range(n_dp))]
+        ]
+
     far = [1, 2, 3] if mirror else list(range(n_tp - 1, 0, -1))
     routed = [(a, b, 0) for a in reversed(range(n_ctx)) for b in reversed(range(n_dp)) if a + b]
     group = [(a, 0, e) for e in far + [0] for a in reversed(range(n_ctx)) if a + e]
     across = [(0, b, 0) for b in range(1, n_dp)]
 
+    for e in range(n_tp):
+        rows_recv[e, n_ctx:] = jnp.zeros((plane - n_ctx, rows, feats), BF16)
     barrier = pltpu.get_barrier_semaphore()
+    for k in range(n_tp - 1, 0, -1):
+
+        @pl.when(p + k < n_tp)
+        def _():
+            for place in whole_plane(k):
+                pl.semaphore_signal(
+                    barrier, inc=1, device_id=place, device_id_type=pl.DeviceIdType.MESH
+                )
+
+
     for o in routed:
         pl.semaphore_signal(
             barrier, inc=1, device_id=device(o), device_id_type=pl.DeviceIdType.MESH
         )
-    for k in range(1, n_tp):
-
-        @pl.when(p + k < n_tp)
-        def _():
-            pl.semaphore_signal(
-                barrier, inc=1, device_id=along(k), device_id_type=pl.DeviceIdType.MESH
-            )
-
 
     owns = []
     for source, target in (
@@ -429,7 +434,22 @@
             device_id_type=pl.DeviceIdType.MESH,
         ).start()
 
-    pl.semaphore_wait(barrier, len(routed) + p)
+    def chosen(mark, values):
+        wide = jnp.concatenate([mark] * (feats // 128), axis=1)
+        return jnp.sum(jnp.where(wide > 0.5, values.astype(F32), 0.0), axis=0, keepdims=True)
+
+    for g in range(n_dp):
+        picked = []
+        for t in range(steps):
+            for j in range(per):
+                i = (g * per + j) * steps + t
+                value = chosen(mark_ref[i], raw_ref[i])
+                if vocab % ROW_TILE:
+                    value += chosen(rest_mark_ref[i], rest_ref[...])
+                picked.append(value)
+        part_ref[g] = jnp.concatenate(picked, axis=0).astype(BF16)
+
+    pl.semaphore_wait(barrier, len(routed) + plane * p)
     for k in range(1, n_tp):
 
         @pl.when(p >= k)
@@ -440,8 +460,8 @@
 
 
     for o in routed:
-        send(part_ref.at[peer(o)[1]], plane_recv.at[here_plane], done, plane_sem, device(o))
-    plane_recv[here_plane] = part_ref[d]
+        send(part_ref.at[peer(o)[1]], rows_recv.at[p, here_plane], done, plane_sem, device(o))
+    rows_recv[p, here_plane] = part_ref[d]
 
     owns[0].wait()
     owns[1].wait()
@@ -453,11 +473,6 @@
     send(seg_own, seg_mate, done, mate_sem, mate)
     for o in routed:
         send(seg_own, seg_recv.at[here_plane], done, seg_sem, device(o))
-    owns[2].wait()
-    owns[3].wait()
-    for o in across:
-        send(xt_recv.at[d], xt_recv.at[d], done, xt_sem, device(o))
-        send(bt_recv.at[d], bt_recv.at[d], done, bt_sem, device(o))
     picks = []
     for b in range(n_dp):
         target_group = lax.rem(d + b, n_dp)
@@ -472,6 +487,18 @@
         state_send[slot] = state_in[picks[b], pl.ds(first, chans), :]
         send(state_send.at[slot], pair_recv.at[slot], done, pair_sems.at[slot], mate)
 
+    for k in range(n_tp - 1, 0, -1):
+
+        @pl.when(p >= k)
+        def _():
+            for place in whole_plane(-k):
+                send(part_ref.at[place["dp"]], rows_recv.at[p, here_plane], done, line_sems.at[p], place)
+
+    owns[2].wait()
+    owns[3].wait()
+    for o in across:
+        send(xt_recv.at[d], xt_recv.at[d], done, xt_sem, device(o))
+        send(bt_recv.at[d], bt_recv.at[d], done, bt_sem, device(o))
     for i, pair in enumerate(pairs[1:]):
         fetch(*pair, load_sems.at[i + 1], loads)
 
@@ -485,6 +512,10 @@
 
     def flat(value):
         return jnp.sum(jnp.where(head_rows, f32_dot(value, fold), 0.0), axis=0, keepdims=True)
+
+    def full_lanes(value):
+        idle = jnp.zeros((value.shape[0], 128 - value.shape[1]), F32)
+        return jnp.concatenate([value, idle], axis=1) if idle.size else value
 
     def spread(value, first):
         count = value.shape[1]
@@ -499,38 +530,33 @@
     for b in range(n_dp):
         row = pl.ds(picks[b], 1)
         shrink.append(jnp.exp(-jnp.where(parity == 0, seg_mate[row, :], seg_own[row, :])))
-    ones = [jnp.ones((1, tp_heads), F32)] * n_dp
-    shrink = jnp.concatenate(shrink + ones, axis=0)
-    shrink_cols = [
-        jnp.transpose(spread(shrink, lax.rem(c + 2 * a, n_ctx) * heads)) for a in range(half_ctx)
-    ]
+    shrink = full_lanes(jnp.concatenate(shrink, axis=0))
     for slot, (a, b) in enumerate(blocks):
         drain(pair_recv.at[slot], pair_sems.at[slot])
         first = pl.multiple_of(lax.rem(c + 2 * a, n_ctx) * chans, chans)
-        here = state_in[picks[b], pl.ds(first, chans), :].astype(F32)
-        there = pair_recv[slot].astype(F32)
-        factor = shrink_cols[a][:, b : b + 1]
-        even = jnp.where(parity == 0, here, there)
-        odd = jnp.where(parity == 0, there, here)
-        added = (factor * even + odd).astype(BF16)
+        turned = pltpu.roll(shrink, 128 - lax.rem(c + 2 * a, n_ctx) * heads, 1)
+        sums = pair_send.at[slot] if a + b else state_recv.at[d * half_ctx + lax.div(c, 2)]
+        for h in range(heads):
+            spot = pl.ds(h * dim, dim)
+            factor = turned[b : b + 1, h : h + 1]
+            here = state_in[picks[b], pl.ds(pl.multiple_of(first + h * dim, dim), dim), :].astype(F32)
+            there = pair_recv[slot, spot, :].astype(F32)
+            left = jnp.broadcast_to(jnp.where(parity == 0, factor, 1.0), here.shape)
+            right = jnp.broadcast_to(jnp.where(parity == 0, 1.0, factor), here.shape)
+            sums[spot, :] = (left * here + right * there).astype(BF16)
         target = state_recv.at[d * half_ctx + lax.div(c, 2)]
         if a + b:
-            pair_send[slot] = added
             send(pair_send.at[slot], target, done, state_sem, device((2 * a, b, 0)))
-        else:
-            state_recv[d * half_ctx + lax.div(c, 2)] = added
-
-    drain(plane_recv.at[pl.ds(0, plane - 1)], plane_sem)
+
+    drain(rows_recv.at[p, pl.ds(0, plane - 1)], plane_sem)
+    def rows_of(e, i):
+        piece = rows_recv[e, i].astype(F32)
+        for g in range(1, n_dp):
+            piece += rows_recv[e, g * n_ctx + i].astype(F32)
+        return piece
+
     for i in range(n_ctx):
-        piece = plane_recv[i].astype(F32)
-        for g in range(1, n_dp):
-            piece += plane_recv[g * n_ctx + i].astype(F32)
-        line_send[i] = piece.astype(BF16)
-    for k in range(n_tp - 1, 0, -1):
-
-        @pl.when(p >= k)
-        def _():
-            send(line_send, line_recv.at[p], done, line_sems.at[p], along(-k))
+        line_send[i] = rows_of(p, i).astype(BF16)
 
     @pl.when(p < n_tp - 1)
     def _():
@@ -540,14 +566,14 @@
 
         @pl.when(p + k < n_tp)
         def _():
-            send(line_send, line_recv.at[p], done, line_sems.at[p], along(k))
+            send(line_send, rows_recv.at[p, pl.ds(0, n_ctx)], done, line_sems.at[p], along(k))
 
     loads[1].wait()
     tallies = []
 
     def take(values, e):
         spots = [pl.ds(pl.multiple_of((i * n_tp + e) * feats, feats), feats) for i in range(n_ctx)]
-        held = jnp.concatenate([values[i].astype(F32) for i in range(n_ctx)], axis=1)
+        held = jnp.concatenate(values, axis=1)
         gains = jnp.concatenate([gain_ref[:, spot] for spot in spots], axis=1)
         low = (held * gains).astype(BF16)
         weights = jnp.concatenate([wbc[:, spot] for spot in spots], axis=1)
@@ -562,7 +588,7 @@
 
     for load in smalls:
         load.wait()
-    take([line_send[i] for i in range(n_ctx)], p)
+    take([rows_of(p, i) for i in range(n_ctx)], p)
     tap_rows = [flat(cxw_ref[k]) for k in range(taps)]
     bias_row = flat(cxb_ref[...])
     gate_row = flat(gg_ref[...])
@@ -597,12 +623,20 @@
             for k in (2 * m + 1, 2 * m):
                 after = after + seg_recv[holders[j] * n_ctx + k, row, :]
         weights.extend(reversed(ordered))
-    weight_cols = jnp.transpose(spread(jnp.concatenate(weights, axis=0), c * heads))
+    weights = pltpu.roll(full_lanes(jnp.concatenate(weights, axis=0)), 128 - c * heads, 1)
 
     for e in reversed(far):
         there = peer((0, 0, e))[2]
-        drain(line_recv.at[there], line_sems.at[there])
-        take([line_recv[there, i] for i in range(n_ctx)], there)
+
+        @pl.when(there > p)
+        def _():
+            drain(rows_recv.at[there], line_sems.at[there])
+
+        @pl.when(there < p)
+        def _():
+            drain(rows_recv.at[there, pl.ds(0, n_ctx)], line_sems.at[there])
+
+        take([rows_of(there, i) for i in range(n_ctx)], there)
     square, narrow = tallies[0]
     for more, columns in tallies[1:]:
         square, narrow = square + more, narrow + columns
@@ -626,13 +660,16 @@
 
     drain(state_recv.at[pl.ds(0, n_dp * half_ctx - 1)], state_sem)
     for j in range(per):
-        begin = None
-        for m in range(half_ctx):
-            r = j * half_ctx + m
-            term = weight_cols[:, r : r + 1] * state_recv[holders[j] * half_ctx + m].astype(F32)
-            begin = term if begin is None else begin + term
-        start_state[j] = begin
-        start_low[j] = begin.astype(BF16)
+        for h in range(heads):
+            spot = pl.ds(h * dim, dim)
+            begin = None
+            for m in range(half_ctx):
+                r = j * half_ctx + m
+                term = state_recv[holders[j] * half_ctx + m, spot, :].astype(F32)
+                term = jnp.broadcast_to(weights[r : r + 1, h : h + 1], term.shape) * term
+                begin = term if begin is None else begin + term
+            start_state[j, spot, :] = begin
+            start_low[j, spot, :] = begin.astype(BF16)
 
     drain(col_recv.at[pl.ds(0, ring - 1)], col_sem)
     lanes = lax.broadcasted_iota(jnp.int32, (rows, 128), 1)
@@ -703,27 +740,31 @@
     )
     loads[4].wait()
     scaled = (gated * gate_row).astype(BF16)
+    base = lax.div(c, 2) * 2
+    pieces = []
     for e in far + [0]:
-        there = peer((0, 0, e))[2]
-        cuts = [
-            wout[:, pl.ds(pl.multiple_of((a * n_tp + there) * feats, feats), feats)]
-            for a in range(n_ctx)
-        ]
+        chips = [[(2 * m, q, e) for q in range(2)] for m in reversed(range(half_ctx))]
+        pieces.extend(chips if e == far[0] else [sum(chips, [])])
+    for number, piece in enumerate(pieces):
+        there = peer((0, 0, piece[0][2]))[2]
+        goals = [lax.rem(base + m + q, n_ctx) for m, q, _ in piece]
+        cuts = [wout[:, pl.ds(pl.multiple_of((a * n_tp + there) * feats, feats), feats)] for a in goals]
         partial = jnp.dot(scaled, jnp.concatenate(cuts, axis=1), preferred_element_type=F32)
-        for a in range(n_ctx):
-            out_send[e * n_ctx + a] = partial[:, a * feats : (a + 1) * feats].astype(BF16)
-        for a in reversed(range(n_ctx)):
-            if a + e:
-                o = (a, 0, e)
-                spot = e * n_ctx + peer(o)[0]
-                send(out_send.at[spot], out_recv.at[mine], done, out_sem, device(o))
-        if e == far[0]:
+        for i, a in enumerate(goals):
+            out_send[there * n_ctx + a] = partial[:, i * feats : (i + 1) * feats].astype(BF16)
+        for a, (m, _, e) in zip(goals, piece):
+            place = {"ctx": a, "dp": d, "tp": there}
+            spot = there * n_ctx + a
+            if m + e:
+                send(out_send.at[spot], out_recv.at[mine], done, out_sem, place)
+        if number == half_ctx - 1:
             squares = jnp.sum(gated * gated, axis=1, keepdims=True)
             sq_send[...] = jnp.sum(jnp.where(diagonal, squares, 0.0), axis=0, keepdims=True)
             for o in group:
                 send(sq_send, sq_recv.at[mine], done, sq_sem, device(o))
             sq_recv[mine] = sq_send[...]
-    out_recv[mine] = out_send[c]
+    send(out_send.at[p * n_ctx + mate["ctx"]], out_recv.at[mine], done, out_sem, mate)
+    out_recv[mine] = out_send[p * n_ctx + c]
 
     last = jnp.concatenate([at(total, steps - 1)] * steps, axis=0)
     late = by_head(jnp.exp(last - total) * step_size) * xc
@@ -735,8 +776,17 @@
             tall[:, rows + j : rows + j + 1] * start_state[j] + f32_dot(tall[:, :rows], b_own)
         )
 
-    drain(plane_recv.at[pl.ds(0, plane - 1)], done)
-    drain(line_recv.at[pl.ds(0, n_tp - 1)], done)
+    drain(rows_recv.at[p, pl.ds(0, plane - 1)], done)
+    for k in range(1, n_tp):
+
+        @pl.when(p >= k)
+        def _():
+            drain(rows_recv.at[p], done)
+
+        @pl.when(p + k < n_tp)
+        def _():
+            drain(line_send, done)
+
     drain(seg_recv.at[pl.ds(0, plane - 1)], done)
     drain(seg_mate, done)
     drain(state_send, done)
@@ -812,17 +862,17 @@
     anywhere = pl.BlockSpec(memory_space=pl.ANY)
     sem = pltpu.SemaphoreType.DMA
     rest = max(1, vocab % ROW_TILE)
-    part = pl.pallas_call(
-        functools.partial(gather_kernel, steps, slots, n_dp),
-        out_shape=pltpu.VMEM((n_dp, rows, feats), BF16),
-        in_specs=[smem, smem, anywhere],
-        out_specs=vmem,
-        scratch_shapes=[
+    picked = pl.pallas_call(
+        functools.partial(gather_kernel, steps, slots),
+        out_shape=(
             pltpu.VMEM((steps * slots, ROW_TILE, feats), BF16),
             pltpu.VMEM((rest, feats), BF16),
-            sem,
-            sem,
-        ],
+            pltpu.VMEM((steps * slots, ROW_TILE, 128), F32),
+            pltpu.VMEM((steps * slots, rest, 128), F32),
+        ),
+        in_specs=[smem, smem, anywhere],
+        out_specs=(vmem,) * 4,
+        scratch_shapes=[sem, sem],
         name="gather_rows",
     )(token_ids, decode_prompt, embedding)
     wide = 2 * state_n
@@ -840,15 +890,16 @@
     )
     bc_planes = jnp.swapaxes(bc_tail, 0, 1)
     mixed, final = pl.pallas_call(
-        functools.partial(mixer_kernel, sizes),
+        functools.partial(mixer_kernel, sizes, vocab),
         out_shape=(
             pltpu.VMEM((steps, per, feats), BF16),
             pltpu.VMEM((per, chans, state_n), F32),
         ),
-        in_specs=[anywhere, vmem] + [anywhere] * 16,
+        in_specs=[anywhere] + [vmem] * 4 + [anywhere] * 16,
         out_specs=(vmem, vmem),
         scratch_shapes=[
             pltpu.SMEM((slots,), jnp.int32),
+            pltpu.VMEM((n_dp, rows, feats), BF16),
             *[pltpu.VMEM(small.shape, small.dtype) for small in smalls],
             pltpu.VMEM((blocks, chans, state_n), BF16),
             pltpu.VMEM((blocks, chans, state_n), BF16),
@@ -858,9 +909,8 @@
             pltpu.VMEM((per, tp_heads * dim, state_n), BF16),
             pltpu.VMEM((blocks, chans, state_n), BF16),
             pltpu.VMEM((blocks, chans, state_n), BF16),
-            pltpu.VMEM((plane, rows, feats), BF16),
+            pltpu.VMEM((n_tp, plane, rows, feats), BF16),
             pltpu.VMEM((n_ctx, rows, feats), BF16),
-            pltpu.VMEM((n_tp, n_ctx, rows, feats), BF16),
             pltpu.VMEM((plane, per, tp_heads), F32),
             pltpu.VMEM((per, tp_heads), F32),
             pltpu.VMEM((per, tp_heads), F32),
@@ -892,7 +942,7 @@
         name="mixer",
     )(
         decode_prompt,
-        pltpu.with_memory_space_constraint(part, pltpu.VMEM),
+        *[pltpu.with_memory_space_constraint(value, pltpu.VMEM) for value in picked],
         seg_rate,
         x_tail,
         bc_planes,
@@ -928,6 +978,7 @@
         and (heads * dim) % 128 == 0
         and w_bcdt.shape[1] <= 128
         and embedding.shape[0] >= ROW_TILE
+        and args[15].shape[2] <= 128
     )
     if fits:
         return kernel_device(sizes, *args)

time: 24.4 us -> 24.1 us (0.988)
  Pallas kernels: 23.6 us -> 23.2 us
    pallas_call x2, Pallas kernels: 22.7 us -> 22.4 us  [the longest x1 20.9 us: kernel_device(): pl.pallas_call(functools.partial(mixer_kernel, sizes, vocab), out_shape=(...]
where the time goes in v5:
time: 24.1 us; the launch traced here: 23.9 us
  Pallas kernels  23.2 us (96%)
  between operations  0.65 us (3%)
    pallas_call x1, Pallas kernels, kernel_device(): pl.pallas_call(functools.partial(mixer_kernel, sizes, vocab), out_shape=(...  20.9 us
    pallas_call x1, Pallas kernels, kernel_device(): pl.pallas_call(functools.partial(gather_kernel, steps, slots), out_shape=...  1.55 us
    pallas_call x1, Pallas kernels, kernel_device(): pl.pallas_call(tail_kernel, out_shape=(jax.ShapeDtypeStruct(mixed.shape,...  0.82 us

profile of v5, /device:TPU:0, one launch (start us, length us, event | category | flops | bytes accessed | tf_op | source)
XLA Modules:
  0.0 23.9 jit_solution(5609672302911216319)
XLA Ops:
  0.6 1.5 %gather_rows.1 = (bf16[16,8,256]{2,1,0:T(8,128)(2,1)S(1)}, bf16[4,256]{1,0:T(4,128)(2,1)S(1)}, f32[16,8,128]{2,1,0:T(8,128)S(1)}, f32[16,4,128]{2,1,0:T(4,128)S(1)}) custom-call(s32[4,4]{1,0:T(4,128)} %tok_ref.1, s32[4]{0:T(128)} %dec_hbm.1, bf16[25140,256]{1,0:T(8,128)(2,1)} %emb_ref.1), custom_call_target="tpu_custom_call" | custom-call | tf_op jit(solution)/shard_map/gather_rows/pallas_call | solution.py:865
  2.2 20.9 %mixer.1 = (bf16[4,2,256]{2,1,0:T(2,128)(2,1)S(1)}, f32[2,512,128]{2,1,0:T(8,128)S(1)}) custom-call(s32[4]{0:T(128)} %dec_hbm.1, bf16[16,8,256]{2,1,0:T(8,128)(2,1)S(1)} %get-tuple-element.10.raw_ref, bf16[4,256]{1,0:T(4,128)(2,1)S(1)} %get-tuple-element.11.rest_ref, f32[16,8,128]{2,1,0:T(8,128)S(1)} %get-tuple-element.12.mark_ref, ...), custom_call_target="tpu_custom_call" | custom-call | tf_op jit(solution)/shard_map/mixer/pallas_call | solution.py:892
  23.1 0.8 %tail.1 = (bf16[4,2,256]{2,1,0:T(2,128)(2,1)}, f32[2,512,128]{2,1,0:T(8,128)}) custom-call(bf16[4,2,256]{2,1,0:T(2,128)(2,1)S(1)} %get-tuple-element.14.mixed_in, f32[2,512,128]{2,1,0:T(8,128)S(1)} %get-tuple-element.15.final_in), custom_call_target="tpu_custom_call" | custom-call | tf_op jit(solution)/shard_map/tail/pallas_call | solution.py:955

commit v6 on v5

--- a/solution.py
+++ b/solution.py
@@ -189,7 +189,7 @@
     whole = vocab // ROW_TILE * ROW_TILE
     row = tok_ref[t, dec_ref[s]] - lax.axis_index("dp") * vocab
     held = (row >= 0) & (row < whole)
-    start = pl.multiple_of(jnp.where(held, row, 0) // ROW_TILE * ROW_TILE, ROW_TILE)
+    start = pl.multiple_of(lax.bitwise_and(jnp.where(held, row, 0), -ROW_TILE), ROW_TILE)
     return row, held, start
 
 
@@ -306,7 +306,8 @@
     normed_ref,
     xfull,
     bcfull,
-    load_sems,
+    state_load,
+    weight_sem,
     small_sem,
     own_sems,
     pair_sems,
@@ -421,8 +422,8 @@
         load.start()
         into.append(load)
 
-    fetch(*pairs[0], load_sems.at[0], loads)
-    for pair in small_pairs:
+    fetch(*pairs[0], state_load, loads)
+    for pair in small_pairs + pairs[1:2]:
         fetch(*pair, small_sem, smalls)
     def send(source, target, send_sem, recv_sem, place):
         pltpu.make_async_remote_copy(
@@ -499,8 +500,8 @@
     for o in across:
         send(xt_recv.at[d], xt_recv.at[d], done, xt_sem, device(o))
         send(bt_recv.at[d], bt_recv.at[d], done, bt_sem, device(o))
-    for i, pair in enumerate(pairs[1:]):
-        fetch(*pair, load_sems.at[i + 1], loads)
+    for pair in pairs[2:]:
+        fetch(*pair, weight_sem, loads)
 
     fold = (
         lax.broadcasted_iota(jnp.int32, (dim, chans), 0)
@@ -568,7 +569,6 @@
         def _():
             send(line_send, rows_recv.at[p, pl.ds(0, n_ctx)], done, line_sems.at[p], along(k))
 
-    loads[1].wait()
     tallies = []
 
     def take(values, e):
@@ -641,14 +641,14 @@
     for more, columns in tallies[1:]:
         square, narrow = square + more, narrow + columns
     scale = lax.rsqrt(jnp.sum(square, axis=1, keepdims=True) / model + epsilon)
-    padded = jnp.concatenate([narrow * scale, jnp.zeros((rows, 128 - n_cols), F32)], axis=1)
-    col_send[...] = pltpu.roll(padded, lax.rem(n_cols * mine, 128), 1)
+    padded = jnp.concatenate([narrow, jnp.zeros((rows, 128 - n_cols), F32)], axis=1)
+    col_send[...] = pltpu.roll(padded, lax.rem(n_cols * mine, 128), 1) * scale
     for o in group:
         send(col_send, col_recv.at[mine], done, col_sem, device(o))
     col_recv[mine] = col_send[...]
-    loads[2].wait()
+    for load in loads[1:]:
+        load.wait()
     x_rows = nt_dot(normed_ref[...], wzx[half : 2 * half, :]) * scale
-    loads[3].wait()
     z_gate = silu(nt_dot(normed_ref[...], wzx[0:half, :]) * scale)
 
     lead = (taps - 1) * per
@@ -738,7 +738,6 @@
     diagonal = lax.broadcasted_iota(jnp.int32, (rows, 128), 0) == lax.broadcasted_iota(
         jnp.int32, (rows, 128), 1
     )
-    loads[4].wait()
     scaled = (gated * gate_row).astype(BF16)
     base = lax.div(c, 2) * 2
     pieces = []
@@ -927,7 +926,8 @@
             pltpu.VMEM((rows, model), BF16),
             pltpu.VMEM((full_rows, chans), F32),
             pltpu.VMEM((full_rows, wide), F32),
-            sem((5,)),
+            sem,
+            sem,
             sem,
             sem((2,)),
             sem((blocks,)),

time: 24.1 us -> 23.9 us (level)
    pallas_call x1, Pallas kernels: 20.9 us -> 20.6 us  [kernel_device(): pl.pallas_call(functools.partial(mixer_kernel, sizes, vocab), out_shape=(...]
where the time goes in v6:
time: 23.9 us; the launch traced here: 23.7 us
  Pallas kernels  23 us (96%)
  between operations  0.65 us (3%)
    pallas_call x1, Pallas kernels, kernel_device(): pl.pallas_call(functools.partial(mixer_kernel, sizes, vocab), out_shape=(...  20.6 us
    pallas_call x1, Pallas kernels, kernel_device(): pl.pallas_call(functools.partial(gather_kernel, steps, slots), out_shape=...  1.58 us
    pallas_call x1, Pallas kernels, kernel_device(): pl.pallas_call(tail_kernel, out_shape=(jax.ShapeDtypeStruct(mixed.shape,...  0.82 us

profile of v6, /device:TPU:0, one launch (start us, length us, event | category | flops | bytes accessed | tf_op | source)
XLA Modules:
  0.0 23.7 jit_solution(7177560416440593162)
XLA Ops:
  0.6 1.6 %gather_rows.1 = (bf16[16,8,256]{2,1,0:T(8,128)(2,1)S(1)}, bf16[4,256]{1,0:T(4,128)(2,1)S(1)}, f32[16,8,128]{2,1,0:T(8,128)S(1)}, f32[16,4,128]{2,1,0:T(4,128)S(1)}) custom-call(s32[4,4]{1,0:T(4,128)} %tok_ref.1, s32[4]{0:T(128)} %dec_hbm.1, bf16[25140,256]{1,0:T(8,128)(2,1)} %emb_ref.1), custom_call_target="tpu_custom_call" | custom-call | tf_op jit(solution)/shard_map/gather_rows/pallas_call | solution.py:864
  2.2 20.6 %mixer.1 = (bf16[4,2,256]{2,1,0:T(2,128)(2,1)S(1)}, f32[2,512,128]{2,1,0:T(8,128)S(1)}) custom-call(s32[4]{0:T(128)} %dec_hbm.1, bf16[16,8,256]{2,1,0:T(8,128)(2,1)S(1)} %get-tuple-element.10.raw_ref, bf16[4,256]{1,0:T(4,128)(2,1)S(1)} %get-tuple-element.11.rest_ref, f32[16,8,128]{2,1,0:T(8,128)S(1)} %get-tuple-element.12.mark_ref, ...), custom_call_target="tpu_custom_call" | custom-call | tf_op jit(solution)/shard_map/mixer/pallas_call | solution.py:891
  22.8 0.8 %tail.1 = (bf16[4,2,256]{2,1,0:T(2,128)(2,1)}, f32[2,512,128]{2,1,0:T(8,128)}) custom-call(bf16[4,2,256]{2,1,0:T(2,128)(2,1)S(1)} %get-tuple-element.14.mixed_in, f32[2,512,128]{2,1,0:T(8,128)S(1)} %get-tuple-element.15.final_in), custom_call_target="tpu_custom_call" | custom-call | tf_op jit(solution)/shard_map/tail/pallas_call | solution.py:955

commit v7 on v6

--- a/solution.py
+++ b/solution.py
@@ -185,16 +185,16 @@
     pltpu.make_async_copy(ref, ref, sem).wait()
 
 
-def row_place(steps, tok_ref, dec_ref, vocab, s, t):
+def row_place(tok_ref, vocab, s, t):
     whole = vocab // ROW_TILE * ROW_TILE
-    row = tok_ref[t, dec_ref[s]] - lax.axis_index("dp") * vocab
+    row = tok_ref[t, s] - lax.axis_index("dp") * vocab
     held = (row >= 0) & (row < whole)
     start = pl.multiple_of(lax.bitwise_and(jnp.where(held, row, 0), -ROW_TILE), ROW_TILE)
     return row, held, start
 
 
 def gather_kernel(
-    steps, slots, tok_ref, dec_ref, emb_ref, buf, tail, mark, tail_mark, sem, tail_sem
+    steps, slots, tok_ref, emb_ref, buf, tail, mark, tail_mark, sem, tail_sem
 ):
     vocab = emb_ref.shape[0]
     whole = vocab // ROW_TILE * ROW_TILE
@@ -209,7 +209,7 @@
     in_tail = False
     for s in range(slots):
         for t in range(steps):
-            row, held, start = row_place(steps, tok_ref, dec_ref, vocab, s, t)
+            row, held, start = row_place(tok_ref, vocab, s, t)
             i = s * steps + t
 
             @pl.when(held)
@@ -435,6 +435,8 @@
             device_id_type=pl.DeviceIdType.MESH,
         ).start()
 
+    owns[0].wait()
+    owns[1].wait()
     def chosen(mark, values):
         wide = jnp.concatenate([mark] * (feats // 128), axis=1)
         return jnp.sum(jnp.where(wide > 0.5, values.astype(F32), 0.0), axis=0, keepdims=True)
@@ -443,7 +445,7 @@
         picked = []
         for t in range(steps):
             for j in range(per):
-                i = (g * per + j) * steps + t
+                i = dec_ref[g * per + j] * steps + t
                 value = chosen(mark_ref[i], raw_ref[i])
                 if vocab % ROW_TILE:
                     value += chosen(rest_mark_ref[i], rest_ref[...])
@@ -464,8 +466,6 @@
         send(part_ref.at[peer(o)[1]], rows_recv.at[p, here_plane], done, plane_sem, device(o))
     rows_recv[p, here_plane] = part_ref[d]
 
-    owns[0].wait()
-    owns[1].wait()
     parity = lax.rem(c, 2)
     mate = {"ctx": c + 1 - 2 * parity, "dp": d, "tp": p}
     half_ctx = n_ctx // 2
@@ -668,7 +668,6 @@
                 term = state_recv[holders[j] * half_ctx + m, spot, :].astype(F32)
                 term = jnp.broadcast_to(weights[r : r + 1, h : h + 1], term.shape) * term
                 begin = term if begin is None else begin + term
-            start_state[j, spot, :] = begin
             start_low[j, spot, :] = begin.astype(BF16)
 
     drain(col_recv.at[pl.ds(0, ring - 1)], col_sem)
@@ -764,6 +763,17 @@
             sq_recv[mine] = sq_send[...]
     send(out_send.at[p * n_ctx + mate["ctx"]], out_recv.at[mine], done, out_sem, mate)
     out_recv[mine] = out_send[p * n_ctx + c]
+
+    for j in range(per):
+        for h in range(heads):
+            spot = pl.ds(h * dim, dim)
+            begin = None
+            for m in range(half_ctx):
+                r = j * half_ctx + m
+                term = state_recv[holders[j] * half_ctx + m, spot, :].astype(F32)
+                term = jnp.broadcast_to(weights[r : r + 1, h : h + 1], term.shape) * term
+                begin = term if begin is None else begin + term
+            start_state[j, spot, :] = begin
 
     last = jnp.concatenate([at(total, steps - 1)] * steps, axis=0)
     late = by_head(jnp.exp(last - total) * step_size) * xc
@@ -869,11 +879,11 @@
             pltpu.VMEM((steps * slots, ROW_TILE, 128), F32),
             pltpu.VMEM((steps * slots, rest, 128), F32),
         ),
-        in_specs=[smem, smem, anywhere],
+        in_specs=[smem, anywhere],
         out_specs=(vmem,) * 4,
         scratch_shapes=[sem, sem],
         name="gather_rows",
-    )(token_ids, decode_prompt, embedding)
+    )(token_ids, embedding)
     wide = 2 * state_n
     full_rows = -(-(conv_x_weight.shape[0] - 1 + steps) * per // 8) * 8
     smalls = (

time: 23.9 us -> 23.8 us (level)
  no operation moved by 1% of the time
where the time goes in v7:
time: 23.8 us; the launch traced here: 23.6 us
  Pallas kernels  23 us (97%)
  between operations  0.65 us (3%)
    pallas_call x1, Pallas kernels, kernel_device(): pl.pallas_call(functools.partial(mixer_kernel, sizes, vocab), out_shape=(...  20.7 us
    pallas_call x1, Pallas kernels, kernel_device(): pl.pallas_call(functools.partial(gather_kernel, steps, slots), out_shape=...  1.51 us
    pallas_call x1, Pallas kernels, kernel_device(): pl.pallas_call(tail_kernel, out_shape=(jax.ShapeDtypeStruct(mixed.shape,...  0.82 us

profile of v7, /device:TPU:0, one launch (start us, length us, event | category | flops | bytes accessed | tf_op | source)
XLA Modules:
  0.0 23.6 jit_solution(2517646031174470698)
XLA Ops:
  0.6 1.5 %gather_rows.1 = (bf16[16,8,256]{2,1,0:T(8,128)(2,1)S(1)}, bf16[4,256]{1,0:T(4,128)(2,1)S(1)}, f32[16,8,128]{2,1,0:T(8,128)S(1)}, f32[16,4,128]{2,1,0:T(4,128)S(1)}) custom-call(s32[4,4]{1,0:T(4,128)} %tok_ref.1, bf16[25140,256]{1,0:T(8,128)(2,1)} %emb_ref.1), custom_call_target="tpu_custom_call" | custom-call | tf_op jit(solution)/shard_map/gather_rows/pallas_call | solution.py:874
  2.1 20.7 %mixer.1 = (bf16[4,2,256]{2,1,0:T(2,128)(2,1)S(1)}, f32[2,512,128]{2,1,0:T(8,128)S(1)}) custom-call(s32[4]{0:T(128)} %dec_hbm.1, bf16[16,8,256]{2,1,0:T(8,128)(2,1)S(1)} %get-tuple-element.10.raw_ref, bf16[4,256]{1,0:T(4,128)(2,1)S(1)} %get-tuple-element.11.rest_ref, f32[16,8,128]{2,1,0:T(8,128)S(1)} %get-tuple-element.12.mark_ref, ...), custom_call_target="tpu_custom_call" | custom-call | tf_op jit(solution)/shard_map/mixer/pallas_call | solution.py:901
  22.8 0.8 %tail.1 = (bf16[4,2,256]{2,1,0:T(2,128)(2,1)}, f32[2,512,128]{2,1,0:T(8,128)}) custom-call(bf16[4,2,256]{2,1,0:T(2,128)(2,1)S(1)} %get-tuple-element.14.mixed_in, f32[2,512,128]{2,1,0:T(8,128)S(1)} %get-tuple-element.15.final_in), custom_call_target="tpu_custom_call" | custom-call | tf_op jit(solution)/shard_map/tail/pallas_call | solution.py:965

commit v8 on v7

--- a/solution.py
+++ b/solution.py
@@ -368,8 +368,6 @@
     group = [(a, 0, e) for e in far + [0] for a in reversed(range(n_ctx)) if a + e]
     across = [(0, b, 0) for b in range(1, n_dp)]
 
-    for e in range(n_tp):
-        rows_recv[e, n_ctx:] = jnp.zeros((plane - n_ctx, rows, feats), BF16)
     barrier = pltpu.get_barrier_semaphore()
     for k in range(n_tp - 1, 0, -1):
 
@@ -434,6 +432,12 @@
             device_id=place,
             device_id_type=pl.DeviceIdType.MESH,
         ).start()
+
+    for e in range(n_tp - 1):
+
+        @pl.when(e < p)
+        def _():
+            rows_recv[e, n_ctx:] = jnp.zeros((plane - n_ctx, rows, feats), BF16)
 
     owns[0].wait()
     owns[1].wait()

time: 23.8 us -> 23.8 us (level)
  no operation moved by 1% of the time
where the time goes in v8:
time: 23.8 us; the launch traced here: 23.6 us
  Pallas kernels  22.9 us (96%)
  between operations  0.65 us (3%)
    pallas_call x1, Pallas kernels, kernel_device(): pl.pallas_call(functools.partial(mixer_kernel, sizes, vocab), out_shape=(...  20.5 us
    pallas_call x1, Pallas kernels, kernel_device(): pl.pallas_call(functools.partial(gather_kernel, steps, slots), out_shape=...  1.57 us
    pallas_call x1, Pallas kernels, kernel_device(): pl.pallas_call(tail_kernel, out_shape=(jax.ShapeDtypeStruct(mixed.shape,...  0.82 us

profile of v8, /device:TPU:0, one launch (start us, length us, event | category | flops | bytes accessed | tf_op | source)
XLA Modules:
  0.0 23.6 jit_solution(1624427294924031428)
XLA Ops:
  0.6 1.6 %gather_rows.1 = (bf16[16,8,256]{2,1,0:T(8,128)(2,1)S(1)}, bf16[4,256]{1,0:T(4,128)(2,1)S(1)}, f32[16,8,128]{2,1,0:T(8,128)S(1)}, f32[16,4,128]{2,1,0:T(4,128)S(1)}) custom-call(s32[4,4]{1,0:T(4,128)} %tok_ref.1, bf16[25140,256]{1,0:T(8,128)(2,1)} %emb_ref.1), custom_call_target="tpu_custom_call" | custom-call | tf_op jit(solution)/shard_map/gather_rows/pallas_call | solution.py:878
  2.2 20.5 %mixer.1 = (bf16[4,2,256]{2,1,0:T(2,128)(2,1)S(1)}, f32[2,512,128]{2,1,0:T(8,128)S(1)}) custom-call(s32[4]{0:T(128)} %dec_hbm.1, bf16[16,8,256]{2,1,0:T(8,128)(2,1)S(1)} %get-tuple-element.10.raw_ref, bf16[4,256]{1,0:T(4,128)(2,1)S(1)} %get-tuple-element.11.rest_ref, f32[16,8,128]{2,1,0:T(8,128)S(1)} %get-tuple-element.12.mark_ref, ...), custom_call_target="tpu_custom_call" | custom-call | tf_op jit(solution)/shard_map/mixer/pallas_call | solution.py:905
  22.8 0.8 %tail.1 = (bf16[4,2,256]{2,1,0:T(2,128)(2,1)}, f32[2,512,128]{2,1,0:T(8,128)}) custom-call(bf16[4,2,256]{2,1,0:T(2,128)(2,1)S(1)} %get-tuple-element.14.mixed_in, f32[2,512,128]{2,1,0:T(8,128)S(1)} %get-tuple-element.15.final_in), custom_call_target="tpu_custom_call" | custom-call | tf_op jit(solution)/shard_map/tail/pallas_call | solution.py:969
